TPU v7x, 256 devices: a whole 4x4x8 slice. The times are simulated.
256 devices in a mesh: grp: 16 (over x, y), cls: 16 (over z, core).
Axes of the slice: x: 4, y: 4, z: 8, core: 2. Of those that a mesh axis runs over, the one named last changes fastest.
Arguments:
- images: bfloat16 [8192, 512], P('grp'), may hold values from -240 to 240
- labels: int32 [8192], P('grp'), may hold values from 0 to 32767
- taxon_emb: bfloat16 [32768, 512], P('cls'), may hold values from -3 to 3
- node_emb: bfloat16 [8192, 512], P('cls'), may hold values from -3 to 3
- proj: bfloat16 [512, 512], replicated, may hold values from -0.25 to 0.25
- lineage: int32 [32768, 7], P('cls'), may hold values from -1 to 8191, as said below
Outputs:
- loss: float32 [], replicated
- grad_images: bfloat16 [8192, 512], P('grp')
- grad_taxon: bfloat16 [32768, 512], P('cls')
- grad_node: float32 [8192, 512], P('cls')
- grad_proj: float32 [512, 512], replicated
Inputs may be any that keep to these rules, and one draw needn't show every extreme that they name: `lineage`: nodes are numbered in depth-first order; index c of cls holds nodes c * 512 to (c + 1) * 512 - 1 and taxa c * 2048 to (c + 1) * 2048 - 1, taxa in the order of their genera. Row t lists, for each rank l, the node of rank l on the path from a root of the tree down to the taxon's genus, or -1 where that path has no node of rank l. Column 0 is never -1; column 6 is the genus, held by the same index of cls as the taxon; the last node held by each index is the genus of the last taxon it holds.
All inputs are finite; a program needn't handle non-finite values.
Results may differ from a plain program's by a relative error of at most 0.015.
Values may be sent and summed in bfloat16 or wider, within the bound.
A program may use at most 64 MiB of HBM per device.

v0:
```python
import jax
import jax.numpy as jnp
from jax import lax
from jax.sharding import PartitionSpec as P

logit_scale = 0.1


def entering(shard, axis, combine, identity, reverse):
    size, mine = (lax.axis_size(axis), lax.axis_index(axis))
    everything = jax.tree.map(lambda part: lax.all_gather(part, axis), shard)
    start = jax.tree.map(
        lambda part, zero: jnp.broadcast_to(jnp.asarray(zero, part.dtype), part.shape),
        shard,
        identity,
    )

    def step(k, before):
        at = size - 1 - k if reverse else k
        reached = at > mine if reverse else at < mine
        new = combine(before, jax.tree.map(lambda part: part[at], everything))
        return jax.tree.map(lambda a, b: jnp.where(reached, a, b), new, before)

    return lax.fori_loop(0, size, step, start)


def path_combine(earlier, later_part):
    known = later_part[0] > -1.5
    return (
        jnp.where(known, later_part[0], earlier[0]),
        jnp.where(known[:, None], later_part[1], earlier[1]),
    )


def back_combine(earlier, later_part):
    empty = later_part[0] < -0.5
    same_node = earlier[0] == later_part[0]
    merged_ids = jnp.where(empty, earlier[0], later_part[0])
    merged_grads = jnp.where(
        empty[:, None],
        earlier[1],
        jnp.where(same_node[:, None], later_part[1] + earlier[1], later_part[1]),
    )
    return (merged_ids, merged_grads)


def node_terms(rows_lineage, grad_rows, node_base, node_rows):
    node_iota = jnp.arange(node_rows, dtype=jnp.int32)
    counts = jnp.zeros((node_rows, rows_lineage.shape[0]), jnp.float32)
    for column in range(rows_lineage.shape[1]):
        match = (rows_lineage[:, column] - node_base)[None, :] == node_iota[:, None]
        counts = counts + match.astype(jnp.float32)
    own_grads = jnp.dot(counts.astype(jnp.bfloat16), grad_rows, preferred_element_type=jnp.float32)
    remote = ((rows_lineage >= 0) & (rows_lineage < node_base)).astype(jnp.bfloat16)
    far_grads = lax.dot_general(
        remote, grad_rows, (((0,), (0,)), ((), ())), preferred_element_type=jnp.float32
    )
    return (own_grads, far_grads)


def per_device(images, labels, taxon_emb, node_emb, proj, lineage):
    batch_rows = images.shape[0]
    taxa_rows = taxon_emb.shape[0]
    node_rows = node_emb.shape[0]
    feat_width = proj.shape[0]
    levels = lineage.shape[1]
    n_grp = lax.axis_size("grp")
    cls_index = lax.axis_index("cls")
    node_base = cls_index * node_rows
    taxa_base = cls_index * taxa_rows
    node_iota = jnp.arange(node_rows, dtype=jnp.int32)
    local_mask = (lineage >= node_base) & (lineage < node_base + node_rows)
    remote_mask = (lineage >= 0) & (lineage < node_base)
    local_index = jnp.clip(lineage - node_base, 0, node_rows - 1)
    last_ids = lineage[taxa_rows - 1]
    last_local = local_mask[taxa_rows - 1]
    own_ids = jnp.where(last_local | (last_ids < 0), last_ids, -2).astype(jnp.float32)
    own_rows = jnp.where(
        last_local[:, None],
        jnp.take(node_emb, local_index[taxa_rows - 1], axis=0).astype(jnp.float32),
        0.0,
    )
    unknown = (jnp.full((levels,), -2.0, jnp.float32), jnp.zeros((levels, feat_width), jnp.float32))
    prefix_ids, prefix_rows = entering((own_ids, own_rows), "cls", path_combine, unknown, False)
    running = taxon_emb.astype(jnp.float32)
    for column in range(levels):
        picked = jnp.take(node_emb, local_index[:, column], axis=0).astype(jnp.float32)
        distant = jnp.where(remote_mask[:, column : column + 1], prefix_rows[column][None, :], 0.0)
        running = running + jnp.where(local_mask[:, column : column + 1], picked, distant)
    summed = running.astype(jnp.bfloat16)
    protos = jnp.dot(summed, proj, preferred_element_type=jnp.float32).astype(jnp.bfloat16)
    scores = logit_scale * lax.dot_general(
        images, protos, (((1,), (1,)), ((), ())), preferred_element_type=jnp.float32
    )
    class_iota = jnp.arange(taxa_rows, dtype=jnp.int32)
    label_hit = (labels - taxa_base)[:, None] == class_iota[None, :]
    local_label = jnp.sum(jnp.where(label_hit, scores, 0.0), axis=1)
    local_top = jnp.max(scores, axis=1)
    row_top = lax.pmax(local_top, "cls")
    exp_scores = jnp.exp(scores - row_top[:, None])
    row_total, label_score = lax.psum((jnp.sum(exp_scores, axis=1), local_label), "cls")
    loss_part = jnp.sum(row_top + jnp.log(row_total) - label_score)
    loss = lax.psum(loss_part, "grp") / (batch_rows * n_grp)
    weights = (exp_scores / row_total[:, None] - label_hit.astype(jnp.float32)).astype(jnp.bfloat16)
    image_part = logit_scale * jnp.dot(weights, protos, preferred_element_type=jnp.float32)
    grad_images = lax.psum(image_part, "cls").astype(jnp.bfloat16)
    class_part = logit_scale * lax.dot_general(
        weights, images, (((0,), (0,)), ((), ())), preferred_element_type=jnp.float32
    )
    class_grad = lax.psum(class_part, "grp").astype(jnp.bfloat16)
    grad_taxon = lax.dot_general(
        class_grad, proj, (((1,), (1,)), ((), ())), preferred_element_type=jnp.float32
    ).astype(jnp.bfloat16)
    proj_part = lax.dot_general(
        summed, class_grad, (((0,), (0,)), ((), ())), preferred_element_type=jnp.float32
    )
    grad_proj = lax.psum(proj_part, "cls")
    own_grads, far_grads = node_terms(lineage, grad_taxon, node_base, node_rows)
    back_ids = jnp.where(prefix_ids > -0.5, prefix_ids, -1.0)
    back_grads = jnp.where(back_ids[:, None] > -0.5, far_grads, 0.0)
    nothing = (jnp.full((levels,), -1.0, jnp.float32), jnp.zeros((levels, feat_width), jnp.float32))
    recv_ids, recv_grads = entering((back_ids, back_grads), "cls", back_combine, nothing, True)
    local_pos = recv_ids.astype(jnp.int32) - node_base
    pick_rows = (local_pos[None, :] == node_iota[:, None]).astype(jnp.float32)
    own_grads = own_grads + jnp.dot(pick_rows, recv_grads, precision=lax.Precision.HIGHEST)
    return (loss, grad_images, grad_taxon, own_grads, grad_proj)


def solution(mesh):
    in_specs = (P("grp", None), P("grp"), P("cls", None), P("cls", None), P(), P("cls", None))
    out_specs = (P(), P("grp", None), P("cls", None), P("cls", None), P())
    return jax.shard_map(
        per_device, mesh=mesh, in_specs=in_specs, out_specs=out_specs, check_vma=False
    )
```

profile of v0, /device:TPU:1, one launch (start us, length us, event | category | flops | bytes accessed | tf_op | source)
XLA Modules:
  0.0 481.3 jit_solution(10657170608437602682)
XLA Ops:
  7.3 0.9 compare_and_fusion
  8.4 0.9 convert_reduce_fusion
  9.2 0.9 subtract_clamp_fusion
  10.5 21.2 %all-gather.2 = f32[16,1,7]{2,1,0:T(1,128)S(1)} all-gather(f32[1,1,7]{2,1,0:T(1,128)S(1)} %bitcast.117), channel_id=1, replica_groups=mesh['grp'=16,'cls'=16] {'cls'}, dimensions={0}, use_global_device_ids=true | all-gather | bytes 476 | tf_op jit(solution)/shard_map/all_gather | solution.py:11
  32.7 15.2 %all_gather.21 = f32[16,7,512]{2,1,0:T(8,128)S(1)} all-gather(f32[1,7,512]{2,1,0:T(8,128)S(1)} %convert_select_fusion), channel_id=1, replica_groups=mesh['grp'=16,'cls'=16] {'cls'}, dimensions={0}, use_global_device_ids=true | all-gather | bytes 243712 | tf_op jit(solution)/shard_map/all_gather | solution.py:11
  47.8 1.8 while.34
  49.6 7.5 %gather_fusion.3 = bf16[2048,512]{1,0:T(8,128)(2,1)S(1)} fusion(bf16[512,512]{1,0:T(8,128)(2,1)S(1)} %copy-done, s32[2048]{0:T(1024)S(1)} %fusion.18), kind=kCustom, calls=%fused_computation.2.clone | custom fusion | bytes 4202496 | tf_op jit(solution)/shard_map/jit(_take)/gather | solution.py:87
  57.2 9.2 %gather_fusion.2 = bf16[2048,512]{1,0:T(8,128)(2,1)} fusion(bf16[512,512]{1,0:T(8,128)(2,1)S(1)} %copy-done, s32[2048]{0:T(1024)S(1)} %fusion.17), kind=kCustom, calls=%fused_computation.1.clone | custom fusion | bytes 4202496 | tf_op jit(solution)/shard_map/jit(_take)/gather | solution.py:87
  66.3 9.2 %gather_fusion.5 = bf16[2048,512]{1,0:T(8,128)(2,1)} fusion(bf16[512,512]{1,0:T(8,128)(2,1)S(1)} %copy-done, s32[2048]{0:T(1024)S(1)} %fusion.20), kind=kCustom, calls=%fused_computation.4.clone | custom fusion | bytes 4202496 | tf_op jit(solution)/shard_map/jit(_take)/gather | solution.py:87
  75.5 9.2 %gather_fusion.4 = bf16[2048,512]{1,0:T(8,128)(2,1)} fusion(bf16[512,512]{1,0:T(8,128)(2,1)S(1)} %copy-done, s32[2048]{0:T(1024)S(1)} %fusion.19), kind=kCustom, calls=%fused_computation.3.clone | custom fusion | bytes 4202496 | tf_op jit(solution)/shard_map/jit(_take)/gather | solution.py:87
  84.7 9.2 %gather_fusion.7 = bf16[2048,512]{1,0:T(8,128)(2,1)} fusion(bf16[512,512]{1,0:T(8,128)(2,1)S(1)} %copy-done, s32[2048]{0:T(1024)S(1)} %fusion.22), kind=kCustom, calls=%fused_computation.6.clone | custom fusion | bytes 4202496 | tf_op jit(solution)/shard_map/jit(_take)/gather | solution.py:87
  93.9 9.2 %gather_fusion.6 = bf16[2048,512]{1,0:T(8,128)(2,1)} fusion(bf16[512,512]{1,0:T(8,128)(2,1)S(1)} %copy-done, s32[2048]{0:T(1024)S(1)} %fusion.21), kind=kCustom, calls=%fused_computation.5.clone | custom fusion | bytes 4202496 | tf_op jit(solution)/shard_map/jit(_take)/gather | solution.py:87
  103.0 9.2 %gather_fusion.1 = bf16[2048,512]{1,0:T(8,128)(2,1)} fusion(bf16[512,512]{1,0:T(8,128)(2,1)S(1)} %copy-done, s32[2048]{0:T(1024)S(1)} %fusion.16), kind=kCustom, calls=%fused_computation.clone | custom fusion | bytes 4202496 | tf_op jit(solution)/shard_map/jit(_take)/gather | solution.py:87
  112.2 10.8 %add_convert_fusion.1 = bf16[2048,512]{1,0:T(8,128)(2,1)S(1)} fusion(bf16[2048,512]{1,0:T(8,128)(2,1)} %param.14, bf16[2048,512]{1,0:T(8,128)(2,1)} %gather_fusion.7, bf16[2048,512]{1,0:T(8,128)(2,1)} %gather_fusion.6, bf16[2048,512]{1,0:T(8,128)(2,1)} %gather_fusion.5, bf16[2048,512]{1,0:T(8,128)(2,1)} %gather_fusion.4, ...), kind=kLoop, calls=%fused_computation.34 | loop fusion | flops 38797312 | bytes 18931712 | tf_op jit(solution)/shard_map/convert_element_type | solution.py:90
  123.0 1.2 convolution_convert_fusion.1
  124.4 3.2 multiply_reduce_fusion
  127.6 23.0 %pmax.7 = f32[512]{0:T(512)S(1)} all-reduce(f32[512]{0:T(512)S(1)} %get-tuple-element.405), channel_id=1, replica_groups=mesh['grp'=16,'cls'=16] {'cls'}, use_global_device_ids=true, to_apply=%region_3.5 | all-reduce | flops 512 | bytes 4096 | tf_op jit(solution)/shard_map/pmax | solution.py:99
  150.6 3.4 fusion.2
  154.0 25.2 %psum.42 = f32[512]{0:T(512)S(1)} all-reduce(f32[512]{0:T(512)S(1)} %get-tuple-element.335), channel_id=1, replica_groups=mesh['grp'=16,'cls'=16] {'cls'}, use_global_device_ids=true, to_apply=%region_5.7 | all-reduce | flops 512 | bytes 4096 | tf_op jit(solution)/shard_map/psum | solution.py:101
  179.3 4.8 convolution_multiply_fusion.1
  184.0 3.6 convolution_multiply_fusion
  189.1 54.9 %all-reduce.8 = (f32[512]{0:T(512)S(1)}, bf16[512,512]{1,0:T(8,128)(2,1)}, f32[112]{0:T(128)S(1)}) all-reduce(f32[512]{0:T(512)S(1)} %get-tuple-element.336, f32[512,512]{1,0:T(8,128)} %convolution_multiply_fusion.1, f32[112]{0:T(128)S(1)} %fusion.24), channel_id=1, replica_groups=mesh['grp'=16,'cls'=16] {'cls'}, use_global_device_ids=true, to_apply=%region_7.9 | all-reduce | flops 262768 | bytes 1577856 | tf_op jit(solution)/shard_map/psum | solution.py:101
  243.9 0.6 subtract_reduce_fusion
  244.5 101.3 %all-reduce.9 = (f32[]{:T(128)}, bf16[2048,512]{1,0:T(8,128)(2,1)}) all-reduce(f32[]{:T(128)} %subtract_reduce_fusion, f32[2048,512]{1,0:T(8,128)} %convolution_multiply_fusion), channel_id=1, replica_groups=mesh['grp'=16,'cls'=16] {'grp'}, use_global_device_ids=true, to_apply=%region_9.11 | all-reduce | flops 1048577 | bytes 6291464 | tf_op jit(solution)/shard_map/psum | solution.py:103
  345.9 3.9 fusion.27
  349.9 3.0 convolution_convert_fusion
  353.3 30.8 %all-gather.3 = f32[16,7,512]{2,1,0:T(8,128)S(1)} all-gather(f32[1,7,512]{2,1,0:T(8,128)S(1)} %fusion.11), channel_id=3, replica_groups=mesh['grp'=16,'cls'=16] {'cls'}, dimensions={0}, use_global_device_ids=true | all-gather | bytes 243712 | tf_op jit(solution)/shard_map/all_gather | solution.py:11
  384.1 1.8 while.35
  385.9 4.4 fusion.3
  391.0 2.8 convolution_add_fusion
  393.8 77.2 %all-reduce.7.cloned.1.call-done = f32[512,512]{1,0:T(8,128)} async-done(((f32[512,512]{1,0:T(8,128)}), f32[512,512]{1,0:T(8,128)}) %all-reduce.7.cloned.1.call-update) | async-done | bytes 1048592 | tf_op jit(solution)/shard_map/psum | solution.py:117
  471.0 2.3 copy.45
  (152 shorter events, 6.3 us)
Async XLA Ops:
  7.2 24.9 %copy-start = (bf16[512,512]{1,0:T(8,128)(2,1)S(1)}, bf16[512,512]{1,0:T(8,128)(2,1)}, u32[]{:S(2)}) copy-start(bf16[512,512]{1,0:T(8,128)(2,1)} %param.15) | copy-start | bytes 1572868
  7.2 463.9 %all-reduce.7.cloned.1.call-start = ((), (), s32[]{:S(2)}) async-start(), calls=%async_computation | async-start | bytes 2097152 | tf_op jit(solution)/shard_map/psum | solution.py:117
  112.2 10.8 %copy-start.8 = (bf16[512,512]{1,0:T(8,128)(2,1)S(1)}, bf16[512,512]{1,0:T(8,128)(2,1)}, u32[]{:S(2)}) copy-start(bf16[512,512]{1,0:T(8,128)(2,1)} %param.16) | copy-start | bytes 1572868
  122.9 1.3 copy-start.2
  122.9 1.4 copy-start.6
  124.4 26.3 %copy-start.7 = (s32[512]{0:T(512)S(1)}, s32[512]{0:T(512)}, u32[]{:S(2)}) copy-start(s32[512]{0:T(512)} %param.13) | copy-start | bytes 6148
  179.2 4.8 copy-start.1
  184.0 3.6 copy-start.9
  187.7 158.2 %copy-start.3 = (bf16[2048,512]{1,0:T(8,128)(2,1)S(1)}, bf16[2048,512]{1,0:T(8,128)(2,1)}, u32[]{:S(2)}) copy-start(bf16[2048,512]{1,0:T(8,128)(2,1)} %copy-done.2) | copy-start | bytes 6291460
  345.8 4.0 copy-start.5
  352.9 37.5 %copy-start.4 = (bf16[2048,512]{1,0:T(8,128)(2,1)}, bf16[2048,512]{1,0:T(8,128)(2,1)S(1)}, u32[]{:S(2)}) copy-start(bf16[2048,512]{1,0:T(8,128)(2,1)S(1)} %convolution_convert_fusion) | copy-start | bytes 6291460
Sparse Core Ops, SparseCore 0:
  349.9 121.0 all-reduce.6
where the time goes:
time: 482 us; the launch traced here: 481 us
  blocking collectives  272 us (56%)
  waiting for transfers between devices  77.3 us (16%)
  local copies, waits for them, and re-layouts  67 us (14%)
  matrix products  27.3 us (6%)
  other arithmetic  21.2 us (4%)
  between operations  16.8 us (3%)
    psum x1, blocking collectives, per_device(): loss = lax.psum(loss_part, 'grp') / (batch_rows * n_grp)  101 us
    psum x2, blocking collectives, per_device(): lax.psum((jnp.sum(exp_scores, axis=1), local_label), 'cls')  80.1 us
    psum x1, waiting for transfers between devices, per_device(): grad_proj = lax.psum(proj_part, 'cls')  77.2 us
    all_gather x3, blocking collectives, entering(): everything = jax.tree.map(lambda part: lax.all_gather(part, axis), shard)  67.1 us
    gather x7, local copies, waits for them, and re-layouts, per_device(): jnp.take(node_emb, local_index[:, column], axis=0).astype(jnp.float32)  62.5 us
    pmax x1, blocking collectives, per_device(): row_top = lax.pmax(local_top, 'cls')  23 us
    convert_element_type x1, other arithmetic, per_device(): summed = running.astype(jnp.bfloat16)  10.8 us
  transfers between devices with their start and end apart: 1, of which 1 were waited for; matrix products, arithmetic and copies ran while one was open for 3% of the time, Pallas kernels for 0%

commit v1 on v0

v1 whole, which is shorter than its diff:
```python
import jax
import jax.numpy as jnp
from jax import lax
from jax.experimental import pallas as pl
from jax.experimental.pallas import tpu as pltpu
from jax.sharding import PartitionSpec as P

MESH = pl.DeviceIdType.MESH
f32, bf16, i32 = jnp.float32, jnp.bfloat16, jnp.int32
scale = 0.1
E, LEVELS, T, B, N = 512, 7, 2048, 512, 512
NX, NY, NZ, NC = 4, 4, 8, 2
CLS = NZ * NC
GRP = NX * NY
BATCH = B * GRP
NT = (((1,), (1,)), ((), ()))
TN = (((0,), (0,)), ((), ()))


def dot(a, b):
    return jnp.dot(a, b, preferred_element_type=f32)


def dot_nt(a, b):
    return lax.dot_general(a, b, NT, preferred_element_type=f32)


def dot_tn(a, b):
    return lax.dot_general(a, b, TN, preferred_element_type=f32)


def rows(start, size):
    return pl.ds(pl.multiple_of(start, size), size)


def body(
    lin_ref, lab_ref, img_h, tax_h, node_h, proj_h,
    loss_o, gi_o, gt_o, gn_o, gp_o,
    img, tax, node, proj, lin16, cnt, base32, summed, sc32, pb, vv, acc,
    pub, pubs, ids, idss, stat, stats, labt, labs, far, fars, frow,
    us, ucr, uh, uzr, ug, ppb, ppx, ppxs, ppy, pa, lt, ltx, ltxs, lty,
    gp, rb1, tb1, g2, rb2, tb2, gt, gnb, gib, gpb, lossb,
    in_sem, out_sem,
    pub_s, pub_r, ids_s, ids_r, st_s, st_r, lab_s, lab_r, far_s, far_r,
    rs_s, rs_r, ag_s, ag_r, uc_s, uc_r, uz_s, uz_r, ug_s, ug_r,
    px_s, px_r, py_s, py_r, pz_s, pz_r, lx_s, lx_r, ly_s, ly_r,
):
    g = lax.axis_index("grp")
    c = lax.axis_index("cls")
    x, y = g // NY, lax.rem(g, NY)
    z, k = c // NC, lax.rem(c, NC)
    pos = (x, y)

    def at_x(d):
        return (lax.rem(x + d, NX) * NY + y, c)

    def at_y(d):
        return (x * NY + lax.rem(y + d, NY), c)

    def at_z(d):
        return (g, lax.rem(z + d, NZ) * NC + k)

    def at_c(d):
        return (g, lax.rem(c + d, CLS))

    mate = (g, z * NC + (1 - k))
    near = (at_x, at_y)
    started = []

    def rc(src, dst, ss, rs, dev):
        return pltpu.make_async_remote_copy(
            src_ref=src, dst_ref=dst, send_sem=ss, recv_sem=rs, device_id=dev, device_id_type=MESH
        )

    def go(src, dst, ss, rs, dev):
        cp = rc(src, dst, ss, rs, dev)
        cp.start()
        started.append(cp)
        return cp

    def got(dst, ss, rs):
        rc(dst, dst, ss, rs, mate).wait_recv()

    loads = [
        pltpu.make_async_copy(s, d, in_sem.at[i])
        for i, (s, d) in enumerate(((node_h, node), (img_h, img), (proj_h, proj), (tax_h, tax)))
    ]
    for cp in loads:
        cp.start()
    pubs[...] = jnp.zeros_like(pubs)
    fars[...] = jnp.zeros_like(fars)
    idss[...] = jnp.full_like(idss, -1)

    barrier = pltpu.get_barrier_semaphore()

    def greet(d, _):
        pl.semaphore_signal(barrier, inc=1, device_id=at_c(d), device_id_type=MESH)
        return 0

    lax.fori_loop(1, CLS, greet, 0)
    for d in range(1, NX):
        pl.semaphore_signal(barrier, inc=1, device_id=at_x(d), device_id_type=MESH)
    for d in range(1, NY):
        pl.semaphore_signal(barrier, inc=1, device_id=at_y(d), device_id_type=MESH)

    base = c * N
    tbase = c * T
    lin16[...] = jnp.full_like(lin16, -1)
    lin16[0:LEVELS, :] = lin_ref[...]
    lin = lin16[...]
    remote = (lin >= 0) & (lin < base)
    pid = jnp.max(jnp.where(remote, lin, -1), axis=1, keepdims=True)
    rem16 = jnp.where(remote, 1.0, 0.0).astype(bf16)
    cnt[N : N + 16, :] = rem16
    lane_n = lax.broadcasted_iota(i32, (16, N), 1)
    last = lin16[:, T - 128 : T][:, 127:128]
    loads[0].wait()
    sel = jnp.where(last - base == lane_n, 1.0, 0.0).astype(bf16)
    pub[...] = dot(sel, node[...])[0:8].astype(bf16)
    ids[...] = jnp.broadcast_to(pid[0:8], (8, 128))

    pl.semaphore_wait(barrier, CLS - 1 + NX - 1 + NY - 1)

    def up8(r):
        return rows(r * 8, 8)

    def send_pub(d, _):
        @pl.when(c + d < CLS)
        def _():
            rc(pub, pubs.at[up8(c), :], pub_s.at[d], pub_r.at[d], at_c(d)).start()
        return 0

    lax.fori_loop(1, CLS, send_pub, 0)

    def count_block(i, _):
        nid = lax.broadcasted_iota(i32, (32, T), 0) + (i * 32 + base)
        hit = nid == lin16[0:1, :]
        for l in range(1, LEVELS):
            hit = hit | (nid == lin16[l : l + 1, :])
        cnt[rows(i * 32, 32), :] = jnp.where(hit, 1.0, 0.0).astype(bf16)
        return 0

    lax.fori_loop(0, N // 32, count_block, 0)
    loads[1].wait()
    loads[2].wait()
    loads[3].wait()
    vv[...] = dot_nt(img[...], proj[...]).astype(bf16)

    def local_sum(i, _):
        r = rows(i * 256, 256)
        base32[r, :] = tax[r, :].astype(f32) + dot_tn(cnt[0:N, r], node[...])
        return 0

    lax.fori_loop(0, T // 256, local_sum, 0)

    def wait_pub(d, _):
        @pl.when(c >= d)
        def _():
            got(pubs.at[up8(c - d), :], pub_s.at[d], pub_r.at[d])
        return 0

    lax.fori_loop(1, CLS, wait_pub, 0)
    lane = lax.broadcasted_iota(i32, (16, 128), 1)
    want = (pid >> 9) * 8 + lax.broadcasted_iota(i32, (16, 1), 0)
    pick = jnp.where((want == lane) & (pid >= 0), 1.0, 0.0).astype(bf16)
    prefix = dot(pick, pubs[...]).astype(bf16)

    def score_block(i, top):
        r = rows(i * 256, 256)
        s = (base32[r, :] + dot_tn(cnt[N : N + 16, r], prefix)).astype(bf16)
        summed[r, :] = s
        pr = dot(s, proj[...]).astype(bf16)
        st = scale * dot_nt(pr, img[...])
        sc32[r, :] = st
        return jnp.maximum(top, jnp.max(st.reshape(32, 8, B), axis=0))

    top8 = lax.fori_loop(0, T // 256, score_block, jnp.full((8, B), -jnp.inf, f32))
    mtop = jnp.max(top8, axis=0, keepdims=True)
    label = lab_ref[...] - tbase

    def exp_block(i, carry):
        tot, ls = carry
        r = rows(i * 256, 256)
        st = sc32[r, :]
        hit = lax.broadcasted_iota(i32, (256, B), 0) + i * 256 == label
        p = jnp.exp(st - mtop)
        ls = ls + jnp.sum(jnp.where(hit, st, 0.0).reshape(32, 8, B), axis=0)
        tot = tot + jnp.sum(p.reshape(32, 8, B), axis=0)
        sc32[r, :] = p
        pb[r, 0:B] = p.astype(bf16)
        pb[r, B : 2 * B] = jnp.where(hit, 1.0, 0.0).astype(bf16)
        return tot, ls

    zero8 = jnp.zeros((8, B), f32)
    tot8, ls8 = lax.fori_loop(0, T // 256, exp_block, (zero8, zero8))
    tot = jnp.sum(tot8, axis=0, keepdims=True)
    for q in range(4):
        stat[q : q + 1, :] = mtop[:, q * 128 : q * 128 + 128]
        stat[q + 4 : q + 5, :] = tot[:, q * 128 : q * 128 + 128]
    lsum = ls8[:, 0:128] + ls8[:, 128:256] + ls8[:, 256:384] + ls8[:, 384:512]
    labt[...] = jnp.broadcast_to(jnp.sum(lsum, keepdims=True), (8, 128))

    def send_stat(d, _):
        rc(stat, stats.at[c], st_s.at[d], st_r.at[d], at_c(d)).start()
        return 0

    def send_lab(d, _):
        rc(labt, labs.at[c], lab_s.at[d], lab_r.at[d], at_c(d)).start()
        return 0

    def send_ids(d, _):
        @pl.when(c >= d)
        def _():
            rc(ids, idss.at[up8(c), :], ids_s.at[d], ids_r.at[d], at_c(CLS - d)).start()
        return 0

    lax.fori_loop(1, CLS, send_stat, 0)
    lax.fori_loop(1, CLS, send_lab, 0)
    lax.fori_loop(1, CLS, send_ids, 0)
    stats[c] = stat[...]
    labs[c] = labt[...]

    acc[...] = jnp.zeros_like(acc)

    def u_block(i, _):
        r = rows(i * 512, 512)
        acc[...] += dot_tn(summed[r, :], pb[r, :])
        return 0

    lax.fori_loop(0, T // 512, u_block, 0)

    def wait_stat(d, _):
        got(stats.at[lax.rem(c + CLS - d, CLS)], st_s.at[d], st_r.at[d])
        return 0

    lax.fori_loop(1, CLS, wait_stat, 0)
    all_m = stats[:, 0:4, :]
    gtop = jnp.max(all_m, axis=0)
    gtot = jnp.sum(stats[:, 4:8, :] * jnp.exp(all_m - gtop[None]), axis=0)
    fac = jnp.exp(stat[0:4, :] - gtop) / gtot
    for q in range(4):
        frow[:, q * 128 : q * 128 + 128] = fac[q : q + 1, :]
    fr = frow[...]
    ls_here = jnp.sum(gtop + jnp.log(gtot), keepdims=True)
    us[...] = (acc[:, 0:B] * fr - acc[:, B : 2 * B]).astype(bf16)
    other = rows((1 - k) * 256, 256)
    mine = rows(k * 256, 256)
    uc = go(us.at[other, :], ucr, uc_s.at[0], uc_r.at[0], mate)

    def grads(row):
        r = rows(row, 256)
        hit = lax.broadcasted_iota(i32, (256, B), 0) + row == label
        w = (sc32[r, :] * fr - jnp.where(hit, 1.0, 0.0)).astype(bf16)
        gp[r, :] = (scale * dot(w, vv[...])).astype(bf16)

    def q4(v):
        return lax.rem(v, 4)

    def stage(h, s):
        axis = (h + s) % 2
        p = pos[axis]
        n = 128 if s == 0 else 32
        right, left = near[axis](1), near[axis](3)
        src = gp if s == 0 else g2.at[h]
        rb = (rb1 if s == 0 else rb2).at[h]
        tb = (tb1 if s == 0 else tb2).at[h]
        off = 1024 * h if s == 0 else 0
        sem = (h * 2 + s) * 6

        def part(q, half):
            return rows(off + q * (2 * n) + half * n, n)

        def send(ref, i, dev):
            go(ref, rb.at[i], rs_s.at[sem + i], rs_r.at[sem + i], dev)

        def get(i):
            got(rb.at[i], rs_s.at[sem + i], rs_r.at[sem + i])
            return rb[i].astype(f32)

        def own(q, half):
            return src[part(q, half), :].astype(f32)

        def first():
            send(src.at[part(q4(p + 2), 0), :], 0, right)
            send(src.at[part(q4(p + 2), 1), :], 3, left)

        def second():
            send(src.at[part(q4(p + 1), 1), :], 1, right)
            send(src.at[part(q4(p + 3), 0), :], 4, left)

        def third():
            tb[0] = (own(q4(p + 1), 0) + get(0)).astype(bf16)
            send(tb.at[0], 2, right)
            tb[1] = (own(q4(p + 3), 1) + get(3)).astype(bf16)
            send(tb.at[1], 5, left)

        def last():
            a = own(p, 0) + get(4) + get(2)
            b = own(p, 1) + get(1) + get(5)
            return a.astype(bf16), b.astype(bf16)

        return first, second, third, last

    s1 = (stage(0, 0), stage(1, 0))
    s2 = (stage(0, 1), stage(1, 1))
    for h in range(2):
        grads(1024 * h + q4(pos[h] + 2) * 256)
        s1[h][0]()
    for h in range(2):
        grads(1024 * h + q4(pos[h] + 1) * 256)
        grads(1024 * h + q4(pos[h] + 3) * 256)
        s1[h][1]()
    for h in range(2):
        grads(1024 * h + pos[h] * 256)

    got(ucr, uc_s.at[0], uc_r.at[0])
    uh[...] = (us[mine, :].astype(f32) + ucr[...].astype(f32)).astype(bf16)
    for d in range(1, NZ):
        go(uh.at[rows(q8(z + d) * 32, 32), :], uzr.at[z], uz_s.at[d], uz_r.at[d], at_z(d))
    uzr[z] = uh[rows(z * 32, 32), :]

    for h in range(2):
        s1[h][2]()
    for h in range(2):
        a, b = s1[h][3]()
        g2[h, 0:128, :] = a
        g2[h, 128:256, :] = b
        s2[h][0]()
        s2[h][1]()

    for d in range(1, NZ):
        got(uzr.at[q8(z + NZ - d)], uz_s.at[d], uz_r.at[d])
    uslice = uzr[0].astype(f32)
    for d in range(1, NZ):
        uslice = uslice + uzr[d].astype(f32)
    uslice = uslice.astype(bf16)
    slot = rows((k * 8 + z) * 32, 32)
    ug[slot, :] = uslice
    for d in range(1, NZ):
        go(ug.at[slot, :], ug.at[slot, :], ug_s.at[d], ug_r.at[d], at_z(d))
    ppb[...] = (scale * dot(uslice, img[...])).astype(bf16)
    for d in range(1, 4):
        go(ppb, ppx.at[d], px_s.at[d], px_r.at[d], at_x(d))

    def wait_lab(d, _):
        got(labs.at[lax.rem(c + CLS - d, CLS)], lab_s.at[d], lab_r.at[d])
        return 0

    lax.fori_loop(1, CLS, wait_lab, 0)
    lt[...] = ls_here - jnp.sum(labs[...], axis=0)
    for d in range(1, 4):
        go(lt, ltx.at[d], lx_s.at[d], lx_r.at[d], at_x(d))

    for h in range(2):
        s2[h][2]()

    ag = []
    for h in range(2):
        a, b = s2[h][3]()
        axis1, axis2 = h, 1 - h
        start = 1024 * h + pos[axis1] * 256 + pos[axis2] * 64
        gt[rows(start, 32), :] = a
        gt[rows(start + 32, 32), :] = b

        def ag_stage(s, h=h):
            axis = (h + s) % 2
            p = pos[axis]
            n = 128 if s == 0 else 32
            right, left = near[axis](1), near[axis](3)
            off = 1024 * h + (0 if s == 0 else pos[h] * 256)
            sem = (h * 2 + s) * 6

            def part(q, half):
                return gt.at[rows(off + q * (2 * n) + half * n, n), :]

            def send(q, half, i, dev):
                ref = part(q, half)
                go(ref, ref, ag_s.at[sem + i], ag_r.at[sem + i], dev)

            def get(q, half, i):
                got(part(q, half), ag_s.at[sem + i], ag_r.at[sem + i])

            def first():
                send(p, 0, 0, right)
                send(p, 1, 3, left)
                send(p, 1, 1, right)
                send(p, 0, 4, left)

            def second():
                get(q4(p + 3), 0, 0)
                send(q4(p + 3), 0, 2, right)
                get(q4(p + 1), 1, 3)
                send(q4(p + 1), 1, 5, left)

            def last():
                get(q4(p + 3), 1, 1)
                get(q4(p + 1), 0, 4)
                get(q4(p + 2), 0, 2)
                get(q4(p + 2), 1, 5)

            return first, second, last

        ag.append((ag_stage(0), ag_stage(1)))
        ag[h][1][0]()

    for h in range(2):
        ag[h][1][1]()

    for d in range(1, 4):
        got(ppx.at[d], px_s.at[d], px_r.at[d])
        got(ltx.at[d], lx_s.at[d], lx_r.at[d])
    ppxs[...] = (
        ppb[...].astype(f32) + ppx[1].astype(f32) + ppx[2].astype(f32) + ppx[3].astype(f32)
    ).astype(bf16)
    ltxs[...] = lt[...] + ltx[1] + ltx[2] + ltx[3]
    for d in range(1, 4):
        go(ppxs, ppy.at[d], py_s.at[d], py_r.at[d], at_y(d))
        go(ltxs, lty.at[d], ly_s.at[d], ly_r.at[d], at_y(d))

    for h in range(2):
        ag[h][1][2]()
        ag[h][0][0]()

    for d in range(1, NZ):
        got(ug.at[rows((k * 8 + q8(z + NZ - d)) * 32, 32), :], ug_s.at[d], ug_r.at[d])
    go(ug.at[mine, :], ug.at[mine, :], uc_s.at[1], uc_r.at[1], mate)

    for d in range(1, 4):
        got(ppy.at[d], py_s.at[d], py_r.at[d])
        got(lty.at[d], ly_s.at[d], ly_r.at[d])
    pa[slot, :] = (
        ppxs[...].astype(f32) + ppy[1].astype(f32) + ppy[2].astype(f32) + ppy[3].astype(f32)
    ).astype(bf16)
    for d in range(1, NZ):
        go(pa.at[slot, :], pa.at[slot, :], pz_s.at[d], pz_r.at[d], at_z(d))
    total = ltxs[...] + lty[1] + lty[2] + lty[3]
    lossb[...] = total * (1.0 / BATCH)

    for h in range(2):
        ag[h][0][1]()

    got(ug.at[other, :], uc_s.at[1], uc_r.at[1])
    gib[...] = (scale * dot_tn(ug[...], proj[...])).astype(bf16)
    outs = [pltpu.make_async_copy(gib, gi_o, out_sem.at[0])]
    outs[-1].start()

    for d in range(1, NZ):
        got(pa.at[rows((k * 8 + q8(z + NZ - d)) * 32, 32), :], pz_s.at[d], pz_r.at[d])
    go(pa.at[mine, :], pa.at[mine, :], uc_s.at[2], uc_r.at[2], mate)

    for h in range(2):
        ag[h][0][2]()
    outs.append(pltpu.make_async_copy(gt, gt_o, out_sem.at[1]))
    outs[-1].start()

    far[...] = dot(cnt[N : N + 16, :], gt[...])[0:8].astype(bf16)

    def send_far(d, _):
        @pl.when(c >= d)
        def _():
            rc(far, fars.at[up8(c), :], far_s.at[d], far_r.at[d], at_c(CLS - d)).start()
        return 0

    lax.fori_loop(1, CLS, send_far, 0)

    def node_block(i, _):
        r = rows(i * 128, 128)
        gnb[r, :] = dot(cnt[r, :], gt[...])
        return 0

    lax.fori_loop(0, N // 128, node_block, 0)

    got(pa.at[other, :], uc_s.at[2], uc_r.at[2])
    gpb[...] = pa[...].astype(f32)
    outs.append(pltpu.make_async_copy(gpb, gp_o, out_sem.at[2]))
    outs[-1].start()
    outs.append(pltpu.make_async_copy(lossb, loss_o, out_sem.at[3]))
    outs[-1].start()

    def wait_far(d, _):
        @pl.when(c + d < CLS)
        def _():
            got(idss.at[up8(c + d), :], ids_s.at[d], ids_r.at[d])
            got(fars.at[up8(c + d), :], far_s.at[d], far_r.at[d])
        return 0

    lax.fori_loop(1, CLS, wait_far, 0)
    ri = lax.broadcasted_iota(i32, (128, 128), 0)
    ci = lax.broadcasted_iota(i32, (128, 128), 1)
    idrow = jnp.max(jnp.where(ri == ci, idss[...], -1), axis=0, keepdims=True)
    match = lax.broadcasted_iota(i32, (N, 128), 0) + base == idrow
    gnb[...] += dot(jnp.where(match, 1.0, 0.0).astype(bf16), fars[...])
    outs.append(pltpu.make_async_copy(gnb, gn_o, out_sem.at[4]))
    outs[-1].start()

    for cp in started:
        cp.wait_send()

    def drain(d, _):
        rc(stat, stat, st_s.at[d], st_r.at[d], mate).wait_send()
        rc(labt, labt, lab_s.at[d], lab_r.at[d], mate).wait_send()

        @pl.when(c + d < CLS)
        def _():
            rc(pub, pub, pub_s.at[d], pub_r.at[d], mate).wait_send()

        @pl.when(c >= d)
        def _():
            rc(ids, ids, ids_s.at[d], ids_r.at[d], mate).wait_send()
            rc(far, far, far_s.at[d], far_r.at[d], mate).wait_send()

        return 0

    lax.fori_loop(1, CLS, drain, 0)
    for cp in outs:
        cp.wait()


def q8(v):
    return lax.rem(v, NZ)


def per_device(images, labels, taxon_emb, node_emb, proj, lineage):
    dma = pltpu.SemaphoreType.DMA
    vm = pltpu.VMEM
    scratch = [
        vm((B, E), bf16), vm((T, E), bf16), vm((N, E), bf16), vm((E, E), bf16),
        vm((16, T), i32), vm((N + 16, T), bf16), vm((T, E), f32), vm((T, E), bf16),
        vm((T, B), f32), vm((T, 2 * B), bf16), vm((B, E), bf16), vm((E, 2 * B), f32),
        vm((8, E), bf16), vm((CLS * 8, E), bf16), vm((8, 128), i32), vm((CLS * 8, 128), i32),
        vm((8, 128), f32), vm((CLS, 8, 128), f32), vm((8, 128), f32), vm((CLS, 8, 128), f32),
        vm((8, E), bf16), vm((CLS * 8, E), bf16), vm((1, B), f32),
        vm((E, B), bf16), vm((256, B), bf16), vm((256, B), bf16), vm((NZ, 32, B), bf16),
        vm((E, B), bf16), vm((32, E), bf16), vm((4, 32, E), bf16), vm((32, E), bf16),
        vm((4, 32, E), bf16), vm((E, E), bf16), vm((8, 128), f32), vm((4, 8, 128), f32),
        vm((8, 128), f32), vm((4, 8, 128), f32),
        vm((T, E), bf16), vm((2, 6, 128, E), bf16), vm((2, 2, 128, E), bf16),
        vm((2, 256, E), bf16), vm((2, 6, 32, E), bf16), vm((2, 2, 32, E), bf16),
        vm((T, E), bf16), vm((N, E), f32), vm((B, E), bf16), vm((E, E), f32), vm((8, 128), f32),
        dma((4,)), dma((5,)),
    ]
    scratch += [dma((CLS,))] * 10
    scratch += [dma((24,))] * 4
    scratch += [dma((3,))] * 2 + [dma((NZ,))] * 4
    scratch += [dma((4,))] * 4 + [dma((NZ,))] * 2 + [dma((4,))] * 4
    hbm = pl.BlockSpec(memory_space=pl.ANY)
    vmem = pl.BlockSpec(memory_space=pltpu.VMEM)
    loss, gi, gt, gn, gp = pl.pallas_call(
        body,
        out_shape=(
            jax.ShapeDtypeStruct((8, 128), f32),
            jax.ShapeDtypeStruct((B, E), bf16),
            jax.ShapeDtypeStruct((T, E), bf16),
            jax.ShapeDtypeStruct((N, E), f32),
            jax.ShapeDtypeStruct((E, E), f32),
        ),
        in_specs=[vmem, vmem, hbm, hbm, hbm, hbm],
        out_specs=[hbm] * 5,
        scratch_shapes=scratch,
        compiler_params=pltpu.CompilerParams(
            collective_id=0, has_side_effects=True, vmem_limit_bytes=60 * 1024 * 1024
        ),
    )(lineage.T, labels.reshape(1, B), images, taxon_emb, node_emb, proj)
    return (loss[0, 0], gi, gt, gn, gp)


def solution(mesh):
    in_specs = (P("grp", None), P("grp"), P("cls", None), P("cls", None), P(), P("cls", None))
    out_specs = (P(), P("grp", None), P("cls", None), P("cls", None), P())
    return jax.shard_map(
        per_device, mesh=mesh, in_specs=in_specs, out_specs=out_specs, check_vma=False
    )
```

time: 482 us -> 85.3 us (0.18)
  blocking collectives: 272 us -> 0 us
  waiting for transfers between devices: 77.3 us -> 0 us
  Pallas kernels: 0 us -> 76.3 us
  local copies, waits for them, and re-layouts: 67 us -> 8.2 us
  matrix products: 27.3 us -> 0 us
  other arithmetic: 21.2 us -> 0 us
  between operations: 16.8 us -> 0.65 us
    psum x3 -> x0, blocking collectives: 181 us -> none  [the longest x1 101 us: per_device(): loss = lax.psum(loss_part, 'grp') / (batch_rows * n_grp)]
    psum x1 -> x0, waiting for transfers between devices: 77.2 us -> none  [per_device(): grad_proj = lax.psum(proj_part, 'cls')]
    pallas_call x0 -> x1, Pallas kernels: none -> 76.3 us  [per_device(): pl.pallas_call(body, out_shape=(jax.ShapeDtypeStruct((8, 128), f32), jax....]
    all_gather x3 -> x0, blocking collectives: 67.1 us -> none  [entering(): everything = jax.tree.map(lambda part: lax.all_gather(part, axis), shard)]
    gather x8 -> x0, local copies, waits for them, and re-layouts: 63.1 us -> none  [the longest x7 62.5 us: per_device(): jnp.take(node_emb, local_index[:, column], axis=0).astype(jnp.float32)]
    dot_general x9 -> x0, matrix products: 27.3 us -> none  [the longest x1 4.78 us: per_device(): jnp.dot(weights, protos, preferred_element_type=jnp.float32)]
    pmax x1 -> x0, blocking collectives: 23 us -> none  [per_device(): row_top = lax.pmax(local_top, 'cls')]
    convert_element_type x2 -> x0, other arithmetic: 11.6 us -> none  [the longest x1 10.8 us: per_device(): summed = running.astype(jnp.bfloat16)]
  transfers between devices with their start and end apart: 1 -> 0, of which waited for: 1 -> 0; matrix products, arithmetic and copies ran while one was open for 3% -> 0% of each run, Pallas kernels for 0% -> 0%
where the time goes in v1:
time: 85.3 us; the launch traced here: 85.1 us
  Pallas kernels  76.3 us (89%)
  local copies, waits for them, and re-layouts  8.2 us (10%)
    pallas_call x1, Pallas kernels, per_device(): pl.pallas_call(body, out_shape=(jax.ShapeDtypeStruct((8, 128), f32), jax....  76.3 us
    unnamed x8, local copies, waits for them, and re-layouts  7.01 us

profile of v1, /device:TPU:1, one launch (start us, length us, event | category | flops | bytes accessed | tf_op | source)
XLA Modules:
  0.0 85.1 jit_solution(204564777757977721)
XLA Ops:
  0.6 76.3 %shard_map.101 = (f32[8,128]{1,0:T(8,128)}, bf16[512,512]{1,0:T(8,128)(2,1)}, bf16[2048,512]{1,0:T(8,128)(2,1)}, f32[512,512]{1,0:T(8,128)}, f32[512,512]{1,0:T(8,128)}) custom-call(s32[7,2048]{1,0:T(8,128)} %bitcast.3, s32[1,512]{1,0:T(1,128)} %bitcast.4, bf16[512,512]{1,0:T(8,128)(2,1)} %img_h.1, bf16[2048,512]{1,0:T(8,128)(2,1)} %tax_h.1, ...), custom_call_target="tpu_custom_call" | custom-call | tf_op jit(solution)/shard_map/pallas_call | solution.py:548
  76.9 1.2 %slice.3 = f32[1,1]{1,0:T(1,128)} slice(f32[8,128]{1,0:T(8,128)} %get-tuple-element.10), slice={[0:1], [0:1]} | slice | bytes 8 | tf_op jit(solution)/shard_map/slice | solution.py:564
  78.1 1.9 %copy.15 = bf16[512,512]{1,0:T(8,128)(2,1)} copy(bf16[512,512]{1,0:T(8,128)(2,1)} %get-tuple-element.21) | data formatting | bytes 1048576
  80.0 0.0 copy-start.1
  80.0 0.0 copy-start
  80.0 3.2 %copy.16 = bf16[2048,512]{1,0:T(8,128)(2,1)} copy(bf16[2048,512]{1,0:T(8,128)(2,1)} %get-tuple-element.22) | data formatting | bytes 4194304
  83.2 0.0 copy-done.1
  83.2 1.0 %copy.17 = f32[512,512]{1,0:T(8,128)} copy(f32[512,512]{1,0:T(8,128)S(1)} %copy-done.1) | data formatting | bytes 2097152
  84.1 0.0 copy-done
  84.1 1.0 %copy.18 = f32[512,512]{1,0:T(8,128)} copy(f32[512,512]{1,0:T(8,128)S(1)} %copy-done) | data formatting | bytes 2097152
Async XLA Ops:
  80.0 3.2 %copy-start.1 = (f32[512,512]{1,0:T(8,128)S(1)}, f32[512,512]{1,0:T(8,128)}, u32[]{:S(2)}) copy-start(f32[512,512]{1,0:T(8,128)} %get-tuple-element.23) | copy-start | bytes 3145732
  80.0 4.2 %copy-start = (f32[512,512]{1,0:T(8,128)S(1)}, f32[512,512]{1,0:T(8,128)}, u32[]{:S(2)}) copy-start(f32[512,512]{1,0:T(8,128)} %get-tuple-element.24) | copy-start | bytes 3145732

commit v2 on v1

--- a/solution.py
+++ b/solution.py
@@ -34,16 +34,18 @@
 
 
 def body(
-    lin_ref, lab_ref, img_h, tax_h, node_h, proj_h,
-    loss_o, gi_o, gt_o, gn_o, gp_o,
-    img, tax, node, proj, lin16, cnt, base32, summed, sc32, pb, vv, acc,
+    lin_h, lab_h, img_h, tax_h, node_h, proj_h,
+    lossb, ug, gt, cnt, pa, near_rows, sels, projo,
+    lin_ref, lab_ref, img, tax, node, proj, lin16, base32, summed, sc32, pb, vv, acc, remt,
     pub, pubs, ids, idss, stat, stats, labt, labs, far, fars, frow,
-    us, ucr, uh, uzr, ug, ppb, ppx, ppxs, ppy, pa, lt, ltx, ltxs, lty,
-    gp, rb1, tb1, g2, rb2, tb2, gt, gnb, gib, gpb, lossb,
-    in_sem, out_sem,
+    us, ucr, uh, uzr, ppb, ppx, ppxs, ppy, lt, ltx, ltxs, lty,
+    fx, fxr, fy, fyr,
+    gp, rb1, tb1, g2, rb2, tb2,
+    in_sem,
     pub_s, pub_r, ids_s, ids_r, st_s, st_r, lab_s, lab_r, far_s, far_r,
     rs_s, rs_r, ag_s, ag_r, uc_s, uc_r, uz_s, uz_r, ug_s, ug_r,
     px_s, px_r, py_s, py_r, pz_s, pz_r, lx_s, lx_r, ly_s, ly_r,
+    fx_s, fx_r, fy_s, fy_r,
 ):
     g = lax.axis_index("grp")
     c = lax.axis_index("cls")
@@ -81,9 +83,19 @@
     def got(dst, ss, rs):
         rc(dst, dst, ss, rs, mate).wait_recv()
 
+    def far_first(i):
+        return 8 + (1 - 2 * lax.rem(i, 2)) * ((i + 1) // 2)
+
+    def peers(f):
+        def step(i, _):
+            f(far_first(i))
+            return 0
+
+        lax.fori_loop(0, CLS - 1, step, 0)
+
     loads = [
         pltpu.make_async_copy(s, d, in_sem.at[i])
-        for i, (s, d) in enumerate(((node_h, node), (img_h, img), (proj_h, proj), (tax_h, tax)))
+        for i, (s, d) in enumerate(((lin_h, lin_ref), (node_h, node), (img_h, img), (proj_h, proj), (tax_h, tax), (lab_h, lab_ref)))
     ]
     for cp in loads:
         cp.start()
@@ -106,16 +118,17 @@
     base = c * N
     tbase = c * T
     lin16[...] = jnp.full_like(lin16, -1)
+    loads[0].wait()
     lin16[0:LEVELS, :] = lin_ref[...]
     lin = lin16[...]
     remote = (lin >= 0) & (lin < base)
     pid = jnp.max(jnp.where(remote, lin, -1), axis=1, keepdims=True)
     rem16 = jnp.where(remote, 1.0, 0.0).astype(bf16)
-    cnt[N : N + 16, :] = rem16
     lane_n = lax.broadcasted_iota(i32, (16, N), 1)
     last = lin16[:, T - 128 : T][:, 127:128]
-    loads[0].wait()
+    loads[1].wait()
     sel = jnp.where(last - base == lane_n, 1.0, 0.0).astype(bf16)
+    sels[...] = sel
     pub[...] = dot(sel, node[...])[0:8].astype(bf16)
     ids[...] = jnp.broadcast_to(pid[0:8], (8, 128))
 
@@ -124,13 +137,12 @@
     def up8(r):
         return rows(r * 8, 8)
 
-    def send_pub(d, _):
+    def send_pub(d):
         @pl.when(c + d < CLS)
         def _():
             rc(pub, pubs.at[up8(c), :], pub_s.at[d], pub_r.at[d], at_c(d)).start()
-        return 0
-
-    lax.fori_loop(1, CLS, send_pub, 0)
+
+    peers(send_pub)
 
     def count_block(i, _):
         nid = lax.broadcasted_iota(i32, (32, T), 0) + (i * 32 + base)
@@ -140,18 +152,20 @@
         cnt[rows(i * 32, 32), :] = jnp.where(hit, 1.0, 0.0).astype(bf16)
         return 0
 
-    lax.fori_loop(0, N // 32, count_block, 0)
-    loads[1].wait()
-    loads[2].wait()
-    loads[3].wait()
+    lax.fori_loop(0, N // 32, count_block, 0, unroll=2)
+    eye = lax.broadcasted_iota(i32, (16, 128), 0) == lax.broadcasted_iota(i32, (16, 128), 1)
+    remt[...] = dot_tn(rem16, jnp.where(eye, 1.0, 0.0).astype(bf16)).astype(bf16)
+    for cp in loads[2:]:
+        cp.wait()
+    projo[...] = proj[...]
     vv[...] = dot_nt(img[...], proj[...]).astype(bf16)
 
     def local_sum(i, _):
         r = rows(i * 256, 256)
-        base32[r, :] = tax[r, :].astype(f32) + dot_tn(cnt[0:N, r], node[...])
-        return 0
-
-    lax.fori_loop(0, T // 256, local_sum, 0)
+        base32[r, :] = tax[r, :].astype(f32) + dot_tn(cnt[:, r], node[...])
+        return 0
+
+    lax.fori_loop(0, T // 256, local_sum, 0, unroll=2)
 
     def wait_pub(d, _):
         @pl.when(c >= d)
@@ -160,21 +174,22 @@
         return 0
 
     lax.fori_loop(1, CLS, wait_pub, 0)
-    lane = lax.broadcasted_iota(i32, (16, 128), 1)
-    want = (pid >> 9) * 8 + lax.broadcasted_iota(i32, (16, 1), 0)
-    pick = jnp.where((want == lane) & (pid >= 0), 1.0, 0.0).astype(bf16)
+    lane = lax.broadcasted_iota(i32, (128, 128), 1)
+    pid128 = jnp.concatenate([pid, jnp.full((112, 1), -1, i32)], axis=0)
+    want = (pid128 >> 9) * 8 + lax.broadcasted_iota(i32, (128, 1), 0)
+    pick = jnp.where((want == lane) & (pid128 >= 0), 1.0, 0.0).astype(bf16)
     prefix = dot(pick, pubs[...]).astype(bf16)
 
     def score_block(i, top):
         r = rows(i * 256, 256)
-        s = (base32[r, :] + dot_tn(cnt[N : N + 16, r], prefix)).astype(bf16)
+        s = (base32[r, :] + dot(remt[r, :], prefix)).astype(bf16)
         summed[r, :] = s
         pr = dot(s, proj[...]).astype(bf16)
         st = scale * dot_nt(pr, img[...])
         sc32[r, :] = st
         return jnp.maximum(top, jnp.max(st.reshape(32, 8, B), axis=0))
 
-    top8 = lax.fori_loop(0, T // 256, score_block, jnp.full((8, B), -jnp.inf, f32))
+    top8 = lax.fori_loop(0, T // 256, score_block, jnp.full((8, B), -jnp.inf, f32), unroll=2)
     mtop = jnp.max(top8, axis=0, keepdims=True)
     label = lab_ref[...] - tbase
 
@@ -200,23 +215,18 @@
     lsum = ls8[:, 0:128] + ls8[:, 128:256] + ls8[:, 256:384] + ls8[:, 384:512]
     labt[...] = jnp.broadcast_to(jnp.sum(lsum, keepdims=True), (8, 128))
 
-    def send_stat(d, _):
+    def send_stat(d):
         rc(stat, stats.at[c], st_s.at[d], st_r.at[d], at_c(d)).start()
-        return 0
-
-    def send_lab(d, _):
+
+    def send_lab(d):
         rc(labt, labs.at[c], lab_s.at[d], lab_r.at[d], at_c(d)).start()
-        return 0
-
-    def send_ids(d, _):
+
+    def send_ids(d):
         @pl.when(c >= d)
         def _():
             rc(ids, idss.at[up8(c), :], ids_s.at[d], ids_r.at[d], at_c(CLS - d)).start()
-        return 0
-
-    lax.fori_loop(1, CLS, send_stat, 0)
-    lax.fori_loop(1, CLS, send_lab, 0)
-    lax.fori_loop(1, CLS, send_ids, 0)
+
+    peers(send_stat)
     stats[c] = stat[...]
     labs[c] = labt[...]
 
@@ -247,6 +257,9 @@
     mine = rows(k * 256, 256)
     uc = go(us.at[other, :], ucr, uc_s.at[0], uc_r.at[0], mate)
 
+    peers(send_ids)
+    peers(send_lab)
+
     def grads(row):
         r = rows(row, 256)
         hit = lax.broadcasted_iota(i32, (256, B), 0) + row == label
@@ -354,57 +367,72 @@
     for h in range(2):
         s2[h][2]()
 
-    ag = []
+    def gather(h, s, blk):
+        axis = (h + s) % 2
+        p = pos[axis]
+        right, left = near[axis](1), near[axis](3)
+        if s == 0:
+            step, off, sem = 256, 1024 * h + q4(pos[1 - h] + blk) * 64, (h * 5 + blk) * 6
+        else:
+            step, off, sem = 64, 1024 * h + pos[h] * 256, (h * 5 + 4) * 6
+
+        def part(q, half):
+            return gt.at[rows(off + q * step + half * 32, 32), :]
+
+        def send(q, half, i, dev):
+            ref = part(q, half)
+            go(ref, ref, ag_s.at[sem + i], ag_r.at[sem + i], dev)
+
+        def get(q, half, i):
+            got(part(q, half), ag_s.at[sem + i], ag_r.at[sem + i])
+
+        def first():
+            send(p, 0, 0, right)
+            send(p, 1, 3, left)
+            send(p, 1, 1, right)
+            send(p, 0, 4, left)
+
+        def second():
+            get(q4(p + 3), 0, 0)
+            send(q4(p + 3), 0, 2, right)
+            get(q4(p + 1), 1, 3)
+            send(q4(p + 1), 1, 5, left)
+
+        def third():
+            get(q4(p + 3), 1, 1)
+            get(q4(p + 1), 0, 4)
+
+        def last():
+            get(q4(p + 2), 0, 2)
+            get(q4(p + 2), 1, 5)
+
+        return first, second, third, last
+
+    ag2 = [gather(h, 1, 0) for h in range(2)]
+    ag1 = [[gather(h, 0, b) for b in range(4)] for h in range(2)]
+    fsum = jnp.zeros((128, E), f32)
     for h in range(2):
         a, b = s2[h][3]()
-        axis1, axis2 = h, 1 - h
-        start = 1024 * h + pos[axis1] * 256 + pos[axis2] * 64
+        start = 1024 * h + pos[h] * 256 + pos[1 - h] * 64
         gt[rows(start, 32), :] = a
         gt[rows(start + 32, 32), :] = b
-
-        def ag_stage(s, h=h):
-            axis = (h + s) % 2
-            p = pos[axis]
-            n = 128 if s == 0 else 32
-            right, left = near[axis](1), near[axis](3)
-            off = 1024 * h + (0 if s == 0 else pos[h] * 256)
-            sem = (h * 2 + s) * 6
-
-            def part(q, half):
-                return gt.at[rows(off + q * (2 * n) + half * n, n), :]
-
-            def send(q, half, i, dev):
-                ref = part(q, half)
-                go(ref, ref, ag_s.at[sem + i], ag_r.at[sem + i], dev)
-
-            def get(q, half, i):
-                got(part(q, half), ag_s.at[sem + i], ag_r.at[sem + i])
-
-            def first():
-                send(p, 0, 0, right)
-                send(p, 1, 3, left)
-                send(p, 1, 1, right)
-                send(p, 0, 4, left)
-
-            def second():
-                get(q4(p + 3), 0, 0)
-                send(q4(p + 3), 0, 2, right)
-                get(q4(p + 1), 1, 3)
-                send(q4(p + 1), 1, 5, left)
-
-            def last():
-                get(q4(p + 3), 1, 1)
-                get(q4(p + 1), 0, 4)
-                get(q4(p + 2), 0, 2)
-                get(q4(p + 2), 1, 5)
-
-            return first, second, last
-
-        ag.append((ag_stage(0), ag_stage(1)))
-        ag[h][1][0]()
-
-    for h in range(2):
-        ag[h][1][1]()
+        ag2[h][0]()
+        ag1[h][0][0]()
+        fsum = fsum + dot_tn(remt[rows(start, 32), :], a)
+        fsum = fsum + dot_tn(remt[rows(start + 32, 32), :], b)
+    far[...] = fsum[0:8].astype(bf16)
+
+    def send_far(d):
+        @pl.when(c >= d)
+        def _():
+            rc(far, fars.at[up8(c), :], far_s.at[d], far_r.at[d], at_c(CLS - d)).start()
+
+    peers(send_far)
+
+    for h in range(2):
+        ag2[h][1]()
+    for h in range(2):
+        ag1[h][0][1]()
 
     for d in range(1, 4):
         got(ppx.at[d], px_s.at[d], px_r.at[d])
@@ -418,8 +446,28 @@
         go(ltxs, lty.at[d], ly_s.at[d], ly_r.at[d], at_y(d))
 
     for h in range(2):
-        ag[h][1][2]()
-        ag[h][0][0]()
+        ag2[h][2]()
+        ag1[h][3][0]()
+        ag1[h][1][0]()
+    for h in range(2):
+        ag2[h][3]()
+        ag1[h][2][0]()
+
+    def wait_far(d, _):
+        @pl.when(c + d < CLS)
+        def _():
+            got(idss.at[up8(c + d), :], ids_s.at[d], ids_r.at[d])
+            got(fars.at[up8(c + d), :], far_s.at[d], far_r.at[d])
+        return 0
+
+    lax.fori_loop(1, CLS, wait_far, 0)
+    ri = lax.broadcasted_iota(i32, (128, 128), 0)
+    ci = lax.broadcasted_iota(i32, (128, 128), 1)
+    idrow = jnp.max(jnp.where(ri == ci, idss[...], -1), axis=0, keepdims=True)
+    match = (last == idrow) & (last >= 0)
+    fx[...] = dot(jnp.where(match, 1.0, 0.0).astype(bf16), fars[...])[0:8]
+    for d in range(1, 4):
+        go(fx, fxr.at[d], fx_s.at[d], fx_r.at[d], at_x(d))
 
     for d in range(1, NZ):
         got(ug.at[rows((k * 8 + q8(z + NZ - d)) * 32, 32), :], ug_s.at[d], ug_r.at[d])
@@ -436,62 +484,31 @@
     total = ltxs[...] + lty[1] + lty[2] + lty[3]
     lossb[...] = total * (1.0 / BATCH)
 
-    for h in range(2):
-        ag[h][0][1]()
+    for b in (3, 1):
+        for h in range(2):
+            ag1[h][b][1]()
+    for d in range(1, 4):
+        got(fxr.at[d], fx_s.at[d], fx_r.at[d])
+    fy[...] = fx[...] + fxr[1] + fxr[2] + fxr[3]
+    for d in range(1, 4):
+        go(fy, fyr.at[d], fy_s.at[d], fy_r.at[d], at_y(d))
+    for h in range(2):
+        ag1[h][2][1]()
 
     got(ug.at[other, :], uc_s.at[1], uc_r.at[1])
-    gib[...] = (scale * dot_tn(ug[...], proj[...])).astype(bf16)
-    outs = [pltpu.make_async_copy(gib, gi_o, out_sem.at[0])]
-    outs[-1].start()
 
     for d in range(1, NZ):
         got(pa.at[rows((k * 8 + q8(z + NZ - d)) * 32, 32), :], pz_s.at[d], pz_r.at[d])
     go(pa.at[mine, :], pa.at[mine, :], uc_s.at[2], uc_r.at[2], mate)
 
-    for h in range(2):
-        ag[h][0][2]()
-    outs.append(pltpu.make_async_copy(gt, gt_o, out_sem.at[1]))
-    outs[-1].start()
-
-    far[...] = dot(cnt[N : N + 16, :], gt[...])[0:8].astype(bf16)
-
-    def send_far(d, _):
-        @pl.when(c >= d)
-        def _():
-            rc(far, fars.at[up8(c), :], far_s.at[d], far_r.at[d], at_c(CLS - d)).start()
-        return 0
-
-    lax.fori_loop(1, CLS, send_far, 0)
-
-    def node_block(i, _):
-        r = rows(i * 128, 128)
-        gnb[r, :] = dot(cnt[r, :], gt[...])
-        return 0
-
-    lax.fori_loop(0, N // 128, node_block, 0)
-
+    for d in range(1, 4):
+        got(fyr.at[d], fy_s.at[d], fy_r.at[d])
+    near_rows[...] = fy[...] + fyr[1] + fyr[2] + fyr[3]
+    for b in (0, 3, 1, 2):
+        for h in range(2):
+            ag1[h][b][2]()
+            ag1[h][b][3]()
     got(pa.at[other, :], uc_s.at[2], uc_r.at[2])
-    gpb[...] = pa[...].astype(f32)
-    outs.append(pltpu.make_async_copy(gpb, gp_o, out_sem.at[2]))
-    outs[-1].start()
-    outs.append(pltpu.make_async_copy(lossb, loss_o, out_sem.at[3]))
-    outs[-1].start()
-
-    def wait_far(d, _):
-        @pl.when(c + d < CLS)
-        def _():
-            got(idss.at[up8(c + d), :], ids_s.at[d], ids_r.at[d])
-            got(fars.at[up8(c + d), :], far_s.at[d], far_r.at[d])
-        return 0
-
-    lax.fori_loop(1, CLS, wait_far, 0)
-    ri = lax.broadcasted_iota(i32, (128, 128), 0)
-    ci = lax.broadcasted_iota(i32, (128, 128), 1)
-    idrow = jnp.max(jnp.where(ri == ci, idss[...], -1), axis=0, keepdims=True)
-    match = lax.broadcasted_iota(i32, (N, 128), 0) + base == idrow
-    gnb[...] += dot(jnp.where(match, 1.0, 0.0).astype(bf16), fars[...])
-    outs.append(pltpu.make_async_copy(gnb, gn_o, out_sem.at[4]))
-    outs[-1].start()
 
     for cp in started:
         cp.wait_send()
@@ -512,6 +529,29 @@
         return 0
 
     lax.fori_loop(1, CLS, drain, 0)
+
+
+def finish(lossb, ug, gt, cnt, pa, near_rows, sels, proj, loss_o, gi_o, gt_o, gn_o, gp_o, gib, gnb, gpb, sem):
+    outs = [pltpu.make_async_copy(gt, gt_o, sem.at[0])]
+    outs[-1].start()
+    gpb[...] = pa[...].astype(f32)
+    outs.append(pltpu.make_async_copy(gpb, gp_o, sem.at[1]))
+    outs[-1].start()
+    own = near_rows[...]
+    own = jnp.concatenate([own, jnp.zeros_like(own)], axis=0)
+    hi = own.astype(bf16)
+    lo = (own - hi.astype(f32)).astype(bf16)
+    sel = sels[...]
+    for i in range(2):
+        r = slice(i * 256, i * 256 + 256)
+        at = sel[:, r]
+        gnb[r, :] = dot(cnt[r, :], gt[...]) + dot_tn(at, hi) + dot_tn(at, lo)
+        outs.append(pltpu.make_async_copy(gnb.at[r, :], gn_o.at[r, :], sem.at[2 + i]))
+        outs[-1].start()
+    gib[...] = (scale * dot_tn(ug[...], proj[...])).astype(bf16)
+    outs.append(pltpu.make_async_copy(gib, gi_o, sem.at[4]))
+    outs[-1].start()
+    loss_o[...] = lossb[0:1, 0:1]
     for cp in outs:
         cp.wait()
 
@@ -524,44 +564,58 @@
     dma = pltpu.SemaphoreType.DMA
     vm = pltpu.VMEM
     scratch = [
+        vm((LEVELS, T), i32), vm((1, B), i32),
         vm((B, E), bf16), vm((T, E), bf16), vm((N, E), bf16), vm((E, E), bf16),
-        vm((16, T), i32), vm((N + 16, T), bf16), vm((T, E), f32), vm((T, E), bf16),
-        vm((T, B), f32), vm((T, 2 * B), bf16), vm((B, E), bf16), vm((E, 2 * B), f32),
+        vm((16, T), i32), vm((T, E), f32), vm((T, E), bf16),
+        vm((T, B), f32), vm((T, 2 * B), bf16), vm((B, E), bf16), vm((E, 2 * B), f32), vm((T, 128), bf16),
         vm((8, E), bf16), vm((CLS * 8, E), bf16), vm((8, 128), i32), vm((CLS * 8, 128), i32),
         vm((8, 128), f32), vm((CLS, 8, 128), f32), vm((8, 128), f32), vm((CLS, 8, 128), f32),
         vm((8, E), bf16), vm((CLS * 8, E), bf16), vm((1, B), f32),
         vm((E, B), bf16), vm((256, B), bf16), vm((256, B), bf16), vm((NZ, 32, B), bf16),
-        vm((E, B), bf16), vm((32, E), bf16), vm((4, 32, E), bf16), vm((32, E), bf16),
-        vm((4, 32, E), bf16), vm((E, E), bf16), vm((8, 128), f32), vm((4, 8, 128), f32),
+        vm((32, E), bf16), vm((4, 32, E), bf16), vm((32, E), bf16),
+        vm((4, 32, E), bf16), vm((8, 128), f32), vm((4, 8, 128), f32),
         vm((8, 128), f32), vm((4, 8, 128), f32),
+        vm((8, E), f32), vm((4, 8, E), f32), vm((8, E), f32), vm((4, 8, E), f32),
         vm((T, E), bf16), vm((2, 6, 128, E), bf16), vm((2, 2, 128, E), bf16),
         vm((2, 256, E), bf16), vm((2, 6, 32, E), bf16), vm((2, 2, 32, E), bf16),
-        vm((T, E), bf16), vm((N, E), f32), vm((B, E), bf16), vm((E, E), f32), vm((8, 128), f32),
-        dma((4,)), dma((5,)),
+        dma((6,)),
     ]
     scratch += [dma((CLS,))] * 10
-    scratch += [dma((24,))] * 4
+    scratch += [dma((24,))] * 2 + [dma((60,))] * 2
     scratch += [dma((3,))] * 2 + [dma((NZ,))] * 4
     scratch += [dma((4,))] * 4 + [dma((NZ,))] * 2 + [dma((4,))] * 4
-    hbm = pl.BlockSpec(memory_space=pl.ANY)
+    scratch += [dma((4,))] * 4
+    hbm = pl.BlockSpec(memory_space=pltpu.HBM)
     vmem = pl.BlockSpec(memory_space=pltpu.VMEM)
-    loss, gi, gt, gn, gp = pl.pallas_call(
+    args = (lineage.T, labels.reshape(1, B), images, taxon_emb, node_emb, proj)
+    held = pl.pallas_call(
         body,
         out_shape=(
-            jax.ShapeDtypeStruct((8, 128), f32),
+            vm((8, 128), f32), vm((E, B), bf16), vm((T, E), bf16), vm((N, T), bf16),
+            vm((E, E), bf16), vm((8, E), f32), vm((16, N), bf16), vm((E, E), bf16),
+        ),
+        in_specs=[hbm] * 6,
+        out_specs=[vmem] * 8,
+        scratch_shapes=scratch,
+        compiler_params=pltpu.CompilerParams(
+            collective_id=0, has_side_effects=True, vmem_limit_bytes=46 * 1024 * 1024
+        ),
+    )(*[pltpu.with_memory_space_constraint(a, pltpu.HBM) for a in args])
+    loss, gi, gt, gn, gp = pl.pallas_call(
+        finish,
+        out_shape=(
+            jax.ShapeDtypeStruct((1, 1), f32),
             jax.ShapeDtypeStruct((B, E), bf16),
             jax.ShapeDtypeStruct((T, E), bf16),
             jax.ShapeDtypeStruct((N, E), f32),
             jax.ShapeDtypeStruct((E, E), f32),
         ),
-        in_specs=[vmem, vmem, hbm, hbm, hbm, hbm],
-        out_specs=[hbm] * 5,
-        scratch_shapes=scratch,
-        compiler_params=pltpu.CompilerParams(
-            collective_id=0, has_side_effects=True, vmem_limit_bytes=60 * 1024 * 1024
-        ),
-    )(lineage.T, labels.reshape(1, B), images, taxon_emb, node_emb, proj)
-    return (loss[0, 0], gi, gt, gn, gp)
+        in_specs=[vmem] * 8,
+        out_specs=[vmem] + [hbm] * 4,
+        scratch_shapes=[vm((B, E), bf16), vm((N, E), f32), vm((E, E), f32), dma((5,))],
+        compiler_params=pltpu.CompilerParams(vmem_limit_bytes=12 * 1024 * 1024),
+    )(*held)
+    return (loss.reshape(()), gi, gt, gn, gp)
 
 
 def solution(mesh):

time: 85.3 us -> 74.6 us (0.87)
  local copies, waits for them, and re-layouts: 8.2 us -> 0 us
  Pallas kernels: 76.3 us -> 73.8 us
    unnamed x8 -> x0, local copies, waits for them, and re-layouts: 7.01 us -> none
    pallas_call x1 -> x2, Pallas kernels: 76.3 us -> 73.8 us  [the longest x1 70.4 us: per_device(): pl.pallas_call(body, out_shape=(vm((8, 128), f32), vm((E, B), bf16), vm((...]
    slice x1 -> x0, local copies, waits for them, and re-layouts: 1.19 us -> none  [per_device(): return (loss[0, 0], gi, gt, gn, gp)]
where the time goes in v2:
time: 74.6 us; the launch traced here: 74.5 us
  Pallas kernels  73.8 us (99%)
    pallas_call x1, Pallas kernels, per_device(): pl.pallas_call(body, out_shape=(vm((8, 128), f32), vm((E, B), bf16), vm((...  70.4 us
    pallas_call x1, Pallas kernels, per_device(): pl.pallas_call(finish, out_shape=(jax.ShapeDtypeStruct((1, 1), f32), jax....  3.48 us

profile of v2, /device:TPU:1, one launch (start us, length us, event | category | flops | bytes accessed | tf_op | source)
XLA Modules:
  0.0 74.5 jit_solution(1686436634671960956)
XLA Ops:
  0.6 70.4 %shard_map.101 = (f32[8,128]{1,0:T(8,128)S(1)}, bf16[512,512]{1,0:T(8,128)(2,1)S(1)}, bf16[2048,512]{1,0:T(8,128)(2,1)S(1)}, bf16[512,2048]{1,0:T(8,128)(2,1)S(1...) custom-call(s32[7,2048]{1,0:T(8,128)} %bitcast.3, ...), custom_call_target="tpu_custom_call" | custom-call | tf_op jit(solution)/shard_map/pallas_call | solution.py:591
  71.0 3.5 %shard_map.102 = (f32[1,1]{1,0:T(1,128)}, bf16[512,512]{1,0:T(8,128)(2,1)}, bf16[2048,512]{1,0:T(8,128)(2,1)}, f32[512,512]{1,0:T(8,128)}, f32[512,512]{1,0:T(8,128)}) custom-call(f32[8,128]{1,0:T(8,128)S(1)} %get-tuple-element.18.lossb, bf16[512,512]{1,0:T(8,128)(2,1)S(1)} %get-tuple-element.19.ug, bf16[2048,512]{1,0:T(8,128)(2,1)S(1)} %get-tuple-element.20.gt, ...), custom_call_target="tpu_custom_call" | custom-call | tf_op jit(solution)/shard_map/pallas_call | solution.py:604

commit v3 on v2

--- a/solution.py
+++ b/solution.py
@@ -36,14 +36,13 @@
 def body(
     lin_h, lab_h, img_h, tax_h, node_h, proj_h,
     lossb, ug, gt, cnt, pa, near_rows, sels, projo,
-    lin_ref, lab_ref, img, tax, node, proj, lin16, base32, summed, sc32, pb, vv, acc, remt,
+    lin_ref, lab_ref, ia, tax, node, proj, lin16, base32, summed, sc32, pb, acc, remt, sall, cga, glt, gl, gst, gs,
     pub, pubs, ids, idss, stat, stats, labt, labs, far, fars, frow,
     us, ucr, uh, uzr, ppb, ppx, ppxs, ppy, lt, ltx, ltxs, lty,
     fx, fxr, fy, fyr,
-    gp, rb1, tb1, g2, rb2, tb2,
     in_sem,
     pub_s, pub_r, ids_s, ids_r, st_s, st_r, lab_s, lab_r, far_s, far_r,
-    rs_s, rs_r, ag_s, ag_r, uc_s, uc_r, uz_s, uz_r, ug_s, ug_r,
+    ia_s, ia_r, im_s, im_r, gl_s, gl_r, gs_s, gs_r, ag_s, ag_r, uc_s, uc_r, uz_s, uz_r, ug_s, ug_r,
     px_s, px_r, py_s, py_r, pz_s, pz_r, lx_s, lx_r, ly_s, ly_r,
     fx_s, fx_r, fy_s, fy_r,
 ):
@@ -59,6 +58,9 @@
     def at_y(d):
         return (x * NY + lax.rem(y + d, NY), c)
 
+    def at_g(d):
+        return (lax.rem(g + d, GRP), c)
+
     def at_z(d):
         return (g, lax.rem(z + d, NZ) * NC + k)
 
@@ -92,6 +94,8 @@
             return 0
 
         lax.fori_loop(0, CLS - 1, step, 0)
+
+    img = ia.at[x, y]
 
     loads = [
         pltpu.make_async_copy(s, d, in_sem.at[i])
@@ -110,10 +114,12 @@
         return 0
 
     lax.fori_loop(1, CLS, greet, 0)
-    for d in range(1, NX):
-        pl.semaphore_signal(barrier, inc=1, device_id=at_x(d), device_id_type=MESH)
-    for d in range(1, NY):
-        pl.semaphore_signal(barrier, inc=1, device_id=at_y(d), device_id_type=MESH)
+
+    def greet_grp(d, _):
+        pl.semaphore_signal(barrier, inc=1, device_id=at_g(d), device_id_type=MESH)
+        return 0
+
+    lax.fori_loop(1, GRP, greet_grp, 0)
 
     base = c * N
     tbase = c * T
@@ -132,7 +138,7 @@
     pub[...] = dot(sel, node[...])[0:8].astype(bf16)
     ids[...] = jnp.broadcast_to(pid[0:8], (8, 128))
 
-    pl.semaphore_wait(barrier, CLS - 1 + NX - 1 + NY - 1)
+    pl.semaphore_wait(barrier, CLS - 1 + GRP - 1)
 
     def up8(r):
         return rows(r * 8, 8)
@@ -143,6 +149,80 @@
             rc(pub, pubs.at[up8(c), :], pub_s.at[d], pub_r.at[d], at_c(d)).start()
 
     peers(send_pub)
+
+    def q4(v):
+        return lax.rem(v, 4)
+
+    def images(h, blk):
+        axis = h if blk is None else 1 - h
+        p = pos[axis]
+        right, left = near[axis](1), near[axis](3)
+        sem = (h * 5 + (4 if blk is None else blk)) * 6
+
+        def part(q, half):
+            a, b = (q, pos[1 - h]) if blk is None else (q4(pos[h] + blk), q)
+            i, j = (a, b) if h == 0 else (b, a)
+            return ia.at[i, j, rows(k * 256 + h * 128 + half * 64, 64), :]
+
+        def send(q, half, i, dev):
+            ref = part(q, half)
+            go(ref, ref, ia_s.at[sem + i], ia_r.at[sem + i], dev)
+
+        def get(q, half, i):
+            got(part(q, half), ia_s.at[sem + i], ia_r.at[sem + i])
+
+        return ring(p, right, left, send, get)
+
+    def ring(p, right, left, send, get):
+        def first():
+            send(p, 0, 0, right)
+            send(p, 1, 3, left)
+            send(p, 1, 1, right)
+            send(p, 0, 4, left)
+
+        def second():
+            get(q4(p + 3), 0, 0)
+            send(q4(p + 3), 0, 2, right)
+            get(q4(p + 1), 1, 3)
+            send(q4(p + 1), 1, 5, left)
+
+        def third():
+            get(q4(p + 3), 1, 1)
+            get(q4(p + 1), 0, 4)
+
+        def last():
+            get(q4(p + 2), 0, 2)
+            get(q4(p + 2), 1, 5)
+
+        return first, second, third, last
+
+    def whole(h, blk, core):
+        r = rows(core * 256 + h * 128, 128)
+        q = q4(pos[h] + blk)
+        if blk:
+            return [ia.at[q, :, r, :] if h == 0 else ia.at[:, q, r, :]]
+        o = pos[1 - h]
+        at = [q4(o + d) for d in range(1, 4)]
+        return [ia.at[x, v, r, :] if h == 0 else ia.at[v, y, r, :] for v in at]
+
+    def to_mate(h, blk):
+        for n, ref in enumerate(whole(h, blk, k)):
+            i = h * 6 + (n if blk == 0 else 2 + blk)
+            go(ref, ref, im_s.at[i], im_r.at[i], mate)
+
+    def from_mate(h, blk):
+        for n, ref in enumerate(whole(h, blk, 1 - k)):
+            i = h * 6 + (n if blk == 0 else 2 + blk)
+            got(ref, im_s.at[i], im_r.at[i])
+
+    both = range(2)
+    ia_a = [images(h, None) for h in both]
+    ia_b = [[images(h, b) for b in range(4)] for h in both]
+    loads[2].wait()
+    for h in both:
+        ia_a[h][0]()
+    for h in both:
+        ia_b[h][0][0]()
 
     def count_block(i, _):
         nid = lax.broadcasted_iota(i32, (32, T), 0) + (i * 32 + base)
@@ -155,10 +235,15 @@
     lax.fori_loop(0, N // 32, count_block, 0, unroll=2)
     eye = lax.broadcasted_iota(i32, (16, 128), 0) == lax.broadcasted_iota(i32, (16, 128), 1)
     remt[...] = dot_tn(rem16, jnp.where(eye, 1.0, 0.0).astype(bf16)).astype(bf16)
-    for cp in loads[2:]:
+    for cp in loads[3:]:
         cp.wait()
     projo[...] = proj[...]
-    vv[...] = dot_nt(img[...], proj[...]).astype(bf16)
+    for q in range(4):
+        glt[q : q + 1, :] = lab_ref[:, q * 128 : q * 128 + 128]
+    gl[g] = glt[...]
+
+    def send_gl(d):
+        rc(glt, gl.at[g], gl_s.at[d], gl_r.at[d], at_g(d)).start()
 
     def local_sum(i, _):
         r = rows(i * 256, 256)
@@ -166,6 +251,16 @@
         return 0
 
     lax.fori_loop(0, T // 256, local_sum, 0, unroll=2)
+
+    for h in both:
+        ia_a[h][1]()
+    for h in both:
+        ia_b[h][0][1]()
+    for h in both:
+        ia_a[h][2]()
+        ia_b[h][3][0]()
+        ia_b[h][1][0]()
+    peers(send_gl)
 
     def wait_pub(d, _):
         @pl.when(c >= d)
@@ -230,6 +325,17 @@
     stats[c] = stat[...]
     labs[c] = labt[...]
 
+    for h in both:
+        ia_a[h][3]()
+        ia_b[h][2][0]()
+    for b in (3, 1):
+        for h in both:
+            ia_b[h][b][1]()
+    for h in both:
+        ia_b[h][0][2]()
+        ia_b[h][0][3]()
+        to_mate(h, 0)
+
     acc[...] = jnp.zeros_like(acc)
 
     def u_block(i, _):
@@ -238,6 +344,14 @@
         return 0
 
     lax.fori_loop(0, T // 512, u_block, 0)
+
+    for h in both:
+        ia_b[h][2][1]()
+    for b in (3, 1):
+        for h in both:
+            ia_b[h][b][2]()
+            ia_b[h][b][3]()
+            to_mate(h, b)
 
     def wait_stat(d, _):
         got(stats.at[lax.rem(c + CLS - d, CLS)], st_s.at[d], st_r.at[d])
@@ -252,6 +366,14 @@
         frow[:, q * 128 : q * 128 + 128] = fac[q : q + 1, :]
     fr = frow[...]
     ls_here = jnp.sum(gtop + jnp.log(gtot), keepdims=True)
+    gst[0:4, :] = gtop
+    gst[4:8, :] = 1.0 / gtot
+    gs[g] = gst[...]
+
+    def send_gs(d):
+        rc(gst, gs.at[g], gs_s.at[d], gs_r.at[d], at_g(d)).start()
+
+    peers(send_gs)
     us[...] = (acc[:, 0:B] * fr - acc[:, B : 2 * B]).astype(bf16)
     other = rows((1 - k) * 256, 256)
     mine = rows(k * 256, 256)
@@ -260,86 +382,16 @@
     peers(send_ids)
     peers(send_lab)
 
-    def grads(row):
-        r = rows(row, 256)
-        hit = lax.broadcasted_iota(i32, (256, B), 0) + row == label
-        w = (sc32[r, :] * fr - jnp.where(hit, 1.0, 0.0)).astype(bf16)
-        gp[r, :] = (scale * dot(w, vv[...])).astype(bf16)
-
-    def q4(v):
-        return lax.rem(v, 4)
-
-    def stage(h, s):
-        axis = (h + s) % 2
-        p = pos[axis]
-        n = 128 if s == 0 else 32
-        right, left = near[axis](1), near[axis](3)
-        src = gp if s == 0 else g2.at[h]
-        rb = (rb1 if s == 0 else rb2).at[h]
-        tb = (tb1 if s == 0 else tb2).at[h]
-        off = 1024 * h if s == 0 else 0
-        sem = (h * 2 + s) * 6
-
-        def part(q, half):
-            return rows(off + q * (2 * n) + half * n, n)
-
-        def send(ref, i, dev):
-            go(ref, rb.at[i], rs_s.at[sem + i], rs_r.at[sem + i], dev)
-
-        def get(i):
-            got(rb.at[i], rs_s.at[sem + i], rs_r.at[sem + i])
-            return rb[i].astype(f32)
-
-        def own(q, half):
-            return src[part(q, half), :].astype(f32)
-
-        def first():
-            send(src.at[part(q4(p + 2), 0), :], 0, right)
-            send(src.at[part(q4(p + 2), 1), :], 3, left)
-
-        def second():
-            send(src.at[part(q4(p + 1), 1), :], 1, right)
-            send(src.at[part(q4(p + 3), 0), :], 4, left)
-
-        def third():
-            tb[0] = (own(q4(p + 1), 0) + get(0)).astype(bf16)
-            send(tb.at[0], 2, right)
-            tb[1] = (own(q4(p + 3), 1) + get(3)).astype(bf16)
-            send(tb.at[1], 5, left)
-
-        def last():
-            a = own(p, 0) + get(4) + get(2)
-            b = own(p, 1) + get(1) + get(5)
-            return a.astype(bf16), b.astype(bf16)
-
-        return first, second, third, last
-
-    s1 = (stage(0, 0), stage(1, 0))
-    s2 = (stage(0, 1), stage(1, 1))
-    for h in range(2):
-        grads(1024 * h + q4(pos[h] + 2) * 256)
-        s1[h][0]()
-    for h in range(2):
-        grads(1024 * h + q4(pos[h] + 1) * 256)
-        grads(1024 * h + q4(pos[h] + 3) * 256)
-        s1[h][1]()
-    for h in range(2):
-        grads(1024 * h + pos[h] * 256)
+    for h in both:
+        ia_b[h][2][2]()
+        ia_b[h][2][3]()
+        to_mate(h, 2)
 
     got(ucr, uc_s.at[0], uc_r.at[0])
     uh[...] = (us[mine, :].astype(f32) + ucr[...].astype(f32)).astype(bf16)
     for d in range(1, NZ):
         go(uh.at[rows(q8(z + d) * 32, 32), :], uzr.at[z], uz_s.at[d], uz_r.at[d], at_z(d))
     uzr[z] = uh[rows(z * 32, 32), :]
-
-    for h in range(2):
-        s1[h][2]()
-    for h in range(2):
-        a, b = s1[h][3]()
-        g2[h, 0:128, :] = a
-        g2[h, 128:256, :] = b
-        s2[h][0]()
-        s2[h][1]()
 
     for d in range(1, NZ):
         got(uzr.at[q8(z + NZ - d)], uz_s.at[d], uz_r.at[d])
@@ -364,8 +416,44 @@
     for d in range(1, 4):
         go(lt, ltx.at[d], lx_s.at[d], lx_r.at[d], at_x(d))
 
-    for h in range(2):
-        s2[h][2]()
+    starts = [1024 * h + pos[h] * 256 + pos[1 - h] * 64 for h in both]
+    own = jnp.concatenate([summed[rows(starts[h], 64), :] for h in both], axis=0)
+    pr_own = dot(own, proj[...]).astype(bf16)
+    for b in (0, 3, 1, 2):
+        for h in both:
+            from_mate(h, b)
+
+    def own_scores(j, _):
+        sall[j] = scale * dot_nt(pr_own, ia[j // NY, lax.rem(j, NY)])
+        return 0
+
+    lax.fori_loop(0, GRP, own_scores, 0, unroll=2)
+
+    def wait_gs(d, _):
+        o = lax.rem(g + GRP - d, GRP)
+        got(gl.at[o], gl_s.at[d], gl_r.at[d])
+        got(gs.at[o], gs_s.at[d], gs_r.at[d])
+        return 0
+
+    lax.fori_loop(1, GRP, wait_gs, 0)
+    ti = lax.broadcasted_iota(i32, (128, 1), 0)
+    tid = ti + tbase + jnp.where(ti < 64, starts[0], starts[1] - 64)
+
+    def flat(t, r0):
+        return jnp.concatenate([t[r0 + q : r0 + q + 1, :] for q in range(4)], axis=1)
+
+    cga[...] = jnp.zeros_like(cga)
+
+    def own_grads(j, _):
+        t = gs[j]
+        hit = jnp.where(tid == flat(gl[j], 0), 1.0, 0.0)
+        w = jnp.exp(sall[j] - flat(t, 0)) * flat(t, 4) - hit
+        cga[...] += dot(w.astype(bf16), ia[j // NY, lax.rem(j, NY)])
+        return 0
+
+    lax.fori_loop(0, GRP, own_grads, 0, unroll=2)
+    class_grad = (scale * cga[...]).astype(bf16)
+    gown = dot_nt(class_grad, proj[...]).astype(bf16)
 
     def gather(h, s, blk):
         axis = (h + s) % 2
@@ -386,40 +474,17 @@
         def get(q, half, i):
             got(part(q, half), ag_s.at[sem + i], ag_r.at[sem + i])
 
-        def first():
-            send(p, 0, 0, right)
-            send(p, 1, 3, left)
-            send(p, 1, 1, right)
-            send(p, 0, 4, left)
-
-        def second():
-            get(q4(p + 3), 0, 0)
-            send(q4(p + 3), 0, 2, right)
-            get(q4(p + 1), 1, 3)
-            send(q4(p + 1), 1, 5, left)
-
-        def third():
-            get(q4(p + 3), 1, 1)
-            get(q4(p + 1), 0, 4)
-
-        def last():
-            get(q4(p + 2), 0, 2)
-            get(q4(p + 2), 1, 5)
-
-        return first, second, third, last
+        return ring(p, right, left, send, get)
 
     ag2 = [gather(h, 1, 0) for h in range(2)]
     ag1 = [[gather(h, 0, b) for b in range(4)] for h in range(2)]
     fsum = jnp.zeros((128, E), f32)
     for h in range(2):
-        a, b = s2[h][3]()
-        start = 1024 * h + pos[h] * 256 + pos[1 - h] * 64
-        gt[rows(start, 32), :] = a
-        gt[rows(start + 32, 32), :] = b
+        gt[rows(starts[h], 64), :] = gown[h * 64 : h * 64 + 64]
         ag2[h][0]()
         ag1[h][0][0]()
-        fsum = fsum + dot_tn(remt[rows(start, 32), :], a)
-        fsum = fsum + dot_tn(remt[rows(start + 32, 32), :], b)
+    for h in range(2):
+        fsum = fsum + dot_tn(remt[rows(starts[h], 64), :], gown[h * 64 : h * 64 + 64])
     far[...] = fsum[0:8].astype(bf16)
 
     def send_far(d):
@@ -515,6 +580,8 @@
 
     def drain(d, _):
         rc(stat, stat, st_s.at[d], st_r.at[d], mate).wait_send()
+        rc(glt, glt, gl_s.at[d], gl_r.at[d], mate).wait_send()
+        rc(gst, gst, gs_s.at[d], gs_r.at[d], mate).wait_send()
         rc(labt, labt, lab_s.at[d], lab_r.at[d], mate).wait_send()
 
         @pl.when(c + d < CLS)
@@ -565,9 +632,11 @@
     vm = pltpu.VMEM
     scratch = [
         vm((LEVELS, T), i32), vm((1, B), i32),
-        vm((B, E), bf16), vm((T, E), bf16), vm((N, E), bf16), vm((E, E), bf16),
+        vm((NX, NY, B, E), bf16), vm((T, E), bf16), vm((N, E), bf16), vm((E, E), bf16),
         vm((16, T), i32), vm((T, E), f32), vm((T, E), bf16),
-        vm((T, B), f32), vm((T, 2 * B), bf16), vm((B, E), bf16), vm((E, 2 * B), f32), vm((T, 128), bf16),
+        vm((T, B), f32), vm((T, 2 * B), bf16), vm((E, 2 * B), f32), vm((T, 128), bf16),
+        vm((GRP, 128, B), f32), vm((128, E), f32),
+        vm((8, 128), i32), vm((GRP, 8, 128), i32), vm((8, 128), f32), vm((GRP, 8, 128), f32),
         vm((8, E), bf16), vm((CLS * 8, E), bf16), vm((8, 128), i32), vm((CLS * 8, 128), i32),
         vm((8, 128), f32), vm((CLS, 8, 128), f32), vm((8, 128), f32), vm((CLS, 8, 128), f32),
         vm((8, E), bf16), vm((CLS * 8, E), bf16), vm((1, B), f32),
@@ -576,12 +645,10 @@
         vm((4, 32, E), bf16), vm((8, 128), f32), vm((4, 8, 128), f32),
         vm((8, 128), f32), vm((4, 8, 128), f32),
         vm((8, E), f32), vm((4, 8, E), f32), vm((8, E), f32), vm((4, 8, E), f32),
-        vm((T, E), bf16), vm((2, 6, 128, E), bf16), vm((2, 2, 128, E), bf16),
-        vm((2, 256, E), bf16), vm((2, 6, 32, E), bf16), vm((2, 2, 32, E), bf16),
         dma((6,)),
     ]
     scratch += [dma((CLS,))] * 10
-    scratch += [dma((24,))] * 2 + [dma((60,))] * 2
+    scratch += [dma((60,))] * 2 + [dma((12,))] * 2 + [dma((GRP,))] * 4 + [dma((60,))] * 2
     scratch += [dma((3,))] * 2 + [dma((NZ,))] * 4
     scratch += [dma((4,))] * 4 + [dma((NZ,))] * 2 + [dma((4,))] * 4
     scratch += [dma((4,))] * 4
@@ -598,7 +665,7 @@
         out_specs=[vmem] * 8,
         scratch_shapes=scratch,
         compiler_params=pltpu.CompilerParams(
-            collective_id=0, has_side_effects=True, vmem_limit_bytes=46 * 1024 * 1024
+            collective_id=0, has_side_effects=True, vmem_limit_bytes=52 * 1024 * 1024
         ),
     )(*[pltpu.with_memory_space_constraint(a, pltpu.HBM) for a in args])
     loss, gi, gt, gn, gp = pl.pallas_call(

time: 74.6 us -> 81.7 us (1.095)
  Pallas kernels: 73.8 us -> 81 us
    pallas_call x1, Pallas kernels: 70.4 us -> 77.5 us  [per_device(): pl.pallas_call(body, out_shape=(vm((8, 128), f32), vm((E, B), bf16), vm((...]
where the time goes in v3:
time: 81.7 us; the launch traced here: 81.6 us
  Pallas kernels  81 us (99%)
    pallas_call x1, Pallas kernels, per_device(): pl.pallas_call(body, out_shape=(vm((8, 128), f32), vm((E, B), bf16), vm((...  77.5 us
    pallas_call x1, Pallas kernels, per_device(): pl.pallas_call(finish, out_shape=(jax.ShapeDtypeStruct((1, 1), f32), jax....  3.48 us

profile of v3, /device:TPU:1, one launch (start us, length us, event | category | flops | bytes accessed | tf_op | source)
XLA Modules:
  0.0 81.6 jit_solution(17812273714423271288)
XLA Ops:
  0.6 77.5 %shard_map.101 = (f32[8,128]{1,0:T(8,128)S(1)}, bf16[512,512]{1,0:T(8,128)(2,1)S(1)}, bf16[2048,512]{1,0:T(8,128)(2,1)S(1)}, bf16[512,2048]{1,0:T(8,128)(2,1)S(1...) custom-call(s32[7,2048]{1,0:T(8,128)} %bitcast.3, ...), custom_call_target="tpu_custom_call" | custom-call | tf_op jit(solution)/shard_map/pallas_call | solution.py:658
  78.1 3.5 %shard_map.102 = (f32[1,1]{1,0:T(1,128)}, bf16[512,512]{1,0:T(8,128)(2,1)}, bf16[2048,512]{1,0:T(8,128)(2,1)}, f32[512,512]{1,0:T(8,128)}, f32[512,512]{1,0:T(8,128)}) custom-call(f32[8,128]{1,0:T(8,128)S(1)} %get-tuple-element.18.lossb, bf16[512,512]{1,0:T(8,128)(2,1)S(1)} %get-tuple-element.19.ug, bf16[2048,512]{1,0:T(8,128)(2,1)S(1)} %get-tuple-element.20.gt, ...), custom_call_target="tpu_custom_call" | custom-call | tf_op jit(solution)/shard_map/pallas_call | solution.py:671

commit v4 on v2

--- a/solution.py
+++ b/solution.py
@@ -36,14 +36,14 @@
 def body(
     lin_h, lab_h, img_h, tax_h, node_h, proj_h,
     lossb, ug, gt, cnt, pa, near_rows, sels, projo,
-    lin_ref, lab_ref, img, tax, node, proj, lin16, base32, summed, sc32, pb, vv, acc, remt,
+    lin_ref, lab_ref, ia, tax, node, proj, lin16, base32, summed, sc32, pb, acc, remt, sall, cga, glt, gl, gst, gs,
     pub, pubs, ids, idss, stat, stats, labt, labs, far, fars, frow,
     us, ucr, uh, uzr, ppb, ppx, ppxs, ppy, lt, ltx, ltxs, lty,
     fx, fxr, fy, fyr,
-    gp, rb1, tb1, g2, rb2, tb2,
+    g2, rb2, tb2,
     in_sem,
     pub_s, pub_r, ids_s, ids_r, st_s, st_r, lab_s, lab_r, far_s, far_r,
-    rs_s, rs_r, ag_s, ag_r, uc_s, uc_r, uz_s, uz_r, ug_s, ug_r,
+    ia_s, ia_r, gl_s, gl_r, gs_s, gs_r, rs_s, rs_r, ag_s, ag_r, uc_s, uc_r, uz_s, uz_r, ug_s, ug_r,
     px_s, px_r, py_s, py_r, pz_s, pz_r, lx_s, lx_r, ly_s, ly_r,
     fx_s, fx_r, fy_s, fy_r,
 ):
@@ -93,9 +93,11 @@
 
         lax.fori_loop(0, CLS - 1, step, 0)
 
+    img = ia.at[0, x]
+
     loads = [
         pltpu.make_async_copy(s, d, in_sem.at[i])
-        for i, (s, d) in enumerate(((lin_h, lin_ref), (node_h, node), (img_h, img), (proj_h, proj), (tax_h, tax), (lab_h, lab_ref)))
+        for i, (s, d) in enumerate(((lin_h, lin_ref), (node_h, node), (img_h, img), (img_h, ia.at[1, y]), (proj_h, proj), (tax_h, tax), (lab_h, lab_ref)))
     ]
     for cp in loads:
         cp.start()
@@ -144,6 +146,51 @@
 
     peers(send_pub)
 
+    def q4(v):
+        return lax.rem(v, 4)
+
+    def ring(p, right, left, send, get):
+        def first():
+            send(p, 0, 0, right)
+            send(p, 1, 3, left)
+            send(p, 1, 1, right)
+            send(p, 0, 4, left)
+
+        def second():
+            get(q4(p + 3), 0, 0)
+            send(q4(p + 3), 0, 2, right)
+            get(q4(p + 1), 1, 3)
+            send(q4(p + 1), 1, 5, left)
+
+        def third():
+            get(q4(p + 3), 1, 1)
+            get(q4(p + 1), 0, 4)
+
+        def last():
+            get(q4(p + 2), 0, 2)
+            get(q4(p + 2), 1, 5)
+
+        return first, second, third, last
+
+    def images(h):
+        def part(q, half):
+            return ia.at[h, q, rows(half * 256, 256), :]
+
+        def send(q, half, i, dev):
+            ref = part(q, half)
+            go(ref, ref, ia_s.at[h * 6 + i], ia_r.at[h * 6 + i], dev)
+
+        def get(q, half, i):
+            got(part(q, half), ia_s.at[h * 6 + i], ia_r.at[h * 6 + i])
+
+        return ring(pos[h], near[h](1), near[h](3), send, get)
+
+    both = range(2)
+    lines = [images(h) for h in both]
+    for h in both:
+        loads[2 + h].wait()
+        lines[h][0]()
+
     def count_block(i, _):
         nid = lax.broadcasted_iota(i32, (32, T), 0) + (i * 32 + base)
         hit = nid == lin16[0:1, :]
@@ -155,10 +202,15 @@
     lax.fori_loop(0, N // 32, count_block, 0, unroll=2)
     eye = lax.broadcasted_iota(i32, (16, 128), 0) == lax.broadcasted_iota(i32, (16, 128), 1)
     remt[...] = dot_tn(rem16, jnp.where(eye, 1.0, 0.0).astype(bf16)).astype(bf16)
-    for cp in loads[2:]:
+    for cp in loads[4:]:
         cp.wait()
     projo[...] = proj[...]
-    vv[...] = dot_nt(img[...], proj[...]).astype(bf16)
+    for q in range(4):
+        glt[q : q + 1, :] = lab_ref[:, q * 128 : q * 128 + 128]
+    for h in both:
+        gl[h, pos[h]] = glt[...]
+        for d in range(1, 4):
+            go(glt, gl.at[h, pos[h]], gl_s.at[h * 4 + d], gl_r.at[h * 4 + d], near[h](d))
 
     def local_sum(i, _):
         r = rows(i * 256, 256)
@@ -166,6 +218,9 @@
         return 0
 
     lax.fori_loop(0, T // 256, local_sum, 0, unroll=2)
+
+    for h in both:
+        lines[h][1]()
 
     def wait_pub(d, _):
         @pl.when(c >= d)
@@ -239,6 +294,14 @@
 
     lax.fori_loop(0, T // 512, u_block, 0)
 
+    quarter = [1024 * h + pos[h] * 256 for h in both]
+    for h in both:
+        lines[h][2]()
+        lines[h][3]()
+        pr = dot(summed[rows(quarter[h], 256), :], proj[...]).astype(bf16)
+        for j in range(4):
+            sall[h, j] = scale * dot_nt(pr, ia[h, j])
+
     def wait_stat(d, _):
         got(stats.at[lax.rem(c + CLS - d, CLS)], st_s.at[d], st_r.at[d])
         return 0
@@ -252,6 +315,12 @@
         frow[:, q * 128 : q * 128 + 128] = fac[q : q + 1, :]
     fr = frow[...]
     ls_here = jnp.sum(gtop + jnp.log(gtot), keepdims=True)
+    gst[0:4, :] = gtop
+    gst[4:8, :] = 1.0 / gtot
+    for h in both:
+        gs[h, pos[h]] = gst[...]
+        for d in range(1, 4):
+            go(gst, gs.at[h, pos[h]], gs_s.at[h * 4 + d], gs_r.at[h * 4 + d], near[h](d))
     us[...] = (acc[:, 0:B] * fr - acc[:, B : 2 * B]).astype(bf16)
     other = rows((1 - k) * 256, 256)
     mine = rows(k * 256, 256)
@@ -260,28 +329,32 @@
     peers(send_ids)
     peers(send_lab)
 
-    def grads(row):
-        r = rows(row, 256)
-        hit = lax.broadcasted_iota(i32, (256, B), 0) + row == label
-        w = (sc32[r, :] * fr - jnp.where(hit, 1.0, 0.0)).astype(bf16)
-        gp[r, :] = (scale * dot(w, vv[...])).astype(bf16)
-
-    def q4(v):
-        return lax.rem(v, 4)
-
-    def stage(h, s):
-        axis = (h + s) % 2
+    got(ucr, uc_s.at[0], uc_r.at[0])
+    uh[...] = (us[mine, :].astype(f32) + ucr[...].astype(f32)).astype(bf16)
+    for d in range(1, NZ):
+        go(uh.at[rows(q8(z + d) * 32, 32), :], uzr.at[z], uz_s.at[d], uz_r.at[d], at_z(d))
+    uzr[z] = uh[rows(z * 32, 32), :]
+
+    for h in both:
+        for d in range(1, 4):
+            got(gl.at[h, q4(pos[h] + 4 - d)], gl_s.at[h * 4 + d], gl_r.at[h * 4 + d])
+            got(gs.at[h, q4(pos[h] + 4 - d)], gs_s.at[h * 4 + d], gs_r.at[h * 4 + d])
+
+    def flat(t, r0):
+        return jnp.concatenate([t[r0 + q : r0 + q + 1, :] for q in range(4)], axis=1)
+
+    def stage(h):
+        axis = 1 - h
         p = pos[axis]
-        n = 128 if s == 0 else 32
+        n = 32
         right, left = near[axis](1), near[axis](3)
-        src = gp if s == 0 else g2.at[h]
-        rb = (rb1 if s == 0 else rb2).at[h]
-        tb = (tb1 if s == 0 else tb2).at[h]
-        off = 1024 * h if s == 0 else 0
-        sem = (h * 2 + s) * 6
+        src = g2.at[h]
+        rb = rb2.at[h]
+        tb = tb2.at[h]
+        sem = h * 6
 
         def part(q, half):
-            return rows(off + q * (2 * n) + half * n, n)
+            return rows(q * (2 * n) + half * n, n)
 
         def send(ref, i, dev):
             go(ref, rb.at[i], rs_s.at[sem + i], rs_r.at[sem + i], dev)
@@ -314,57 +387,19 @@
 
         return first, second, third, last
 
-    s1 = (stage(0, 0), stage(1, 0))
-    s2 = (stage(0, 1), stage(1, 1))
-    for h in range(2):
-        grads(1024 * h + q4(pos[h] + 2) * 256)
-        s1[h][0]()
-    for h in range(2):
-        grads(1024 * h + q4(pos[h] + 1) * 256)
-        grads(1024 * h + q4(pos[h] + 3) * 256)
-        s1[h][1]()
-    for h in range(2):
-        grads(1024 * h + pos[h] * 256)
-
-    got(ucr, uc_s.at[0], uc_r.at[0])
-    uh[...] = (us[mine, :].astype(f32) + ucr[...].astype(f32)).astype(bf16)
-    for d in range(1, NZ):
-        go(uh.at[rows(q8(z + d) * 32, 32), :], uzr.at[z], uz_s.at[d], uz_r.at[d], at_z(d))
-    uzr[z] = uh[rows(z * 32, 32), :]
-
-    for h in range(2):
-        s1[h][2]()
-    for h in range(2):
-        a, b = s1[h][3]()
-        g2[h, 0:128, :] = a
-        g2[h, 128:256, :] = b
+    s2 = (stage(0), stage(1))
+    for h in both:
+        tid = lax.broadcasted_iota(i32, (256, 1), 0) + (tbase + quarter[h])
+        for j in range(4):
+            t = gs[h, j]
+            hit = jnp.where(tid == flat(gl[h, j], 0), 1.0, 0.0)
+            w = jnp.exp(sall[h, j] - flat(t, 0)) * flat(t, 4) - hit
+            part = dot(w.astype(bf16), ia[h, j])
+            cga[...] = part if j == 0 else cga[...] + part
+        g2[h] = dot_nt((scale * cga[...]).astype(bf16), proj[...]).astype(bf16)
         s2[h][0]()
         s2[h][1]()
-
-    for d in range(1, NZ):
-        got(uzr.at[q8(z + NZ - d)], uz_s.at[d], uz_r.at[d])
-    uslice = uzr[0].astype(f32)
-    for d in range(1, NZ):
-        uslice = uslice + uzr[d].astype(f32)
-    uslice = uslice.astype(bf16)
-    slot = rows((k * 8 + z) * 32, 32)
-    ug[slot, :] = uslice
-    for d in range(1, NZ):
-        go(ug.at[slot, :], ug.at[slot, :], ug_s.at[d], ug_r.at[d], at_z(d))
-    ppb[...] = (scale * dot(uslice, img[...])).astype(bf16)
-    for d in range(1, 4):
-        go(ppb, ppx.at[d], px_s.at[d], px_r.at[d], at_x(d))
-
-    def wait_lab(d, _):
-        got(labs.at[lax.rem(c + CLS - d, CLS)], lab_s.at[d], lab_r.at[d])
-        return 0
-
-    lax.fori_loop(1, CLS, wait_lab, 0)
-    lt[...] = ls_here - jnp.sum(labs[...], axis=0)
-    for d in range(1, 4):
-        go(lt, ltx.at[d], lx_s.at[d], lx_r.at[d], at_x(d))
-
-    for h in range(2):
+    for h in both:
         s2[h][2]()
 
     def gather(h, s, blk):
@@ -386,27 +421,7 @@
         def get(q, half, i):
             got(part(q, half), ag_s.at[sem + i], ag_r.at[sem + i])
 
-        def first():
-            send(p, 0, 0, right)
-            send(p, 1, 3, left)
-            send(p, 1, 1, right)
-            send(p, 0, 4, left)
-
-        def second():
-            get(q4(p + 3), 0, 0)
-            send(q4(p + 3), 0, 2, right)
-            get(q4(p + 1), 1, 3)
-            send(q4(p + 1), 1, 5, left)
-
-        def third():
-            get(q4(p + 3), 1, 1)
-            get(q4(p + 1), 0, 4)
-
-        def last():
-            get(q4(p + 2), 0, 2)
-            get(q4(p + 2), 1, 5)
-
-        return first, second, third, last
+        return ring(p, right, left, send, get)
 
     ag2 = [gather(h, 1, 0) for h in range(2)]
     ag1 = [[gather(h, 0, b) for b in range(4)] for h in range(2)]
@@ -428,6 +443,29 @@
             rc(far, fars.at[up8(c), :], far_s.at[d], far_r.at[d], at_c(CLS - d)).start()
 
     peers(send_far)
+    for d in range(1, NZ):
+        got(uzr.at[q8(z + NZ - d)], uz_s.at[d], uz_r.at[d])
+    uslice = uzr[0].astype(f32)
+    for d in range(1, NZ):
+        uslice = uslice + uzr[d].astype(f32)
+    uslice = uslice.astype(bf16)
+    slot = rows((k * 8 + z) * 32, 32)
+    ug[slot, :] = uslice
+    for d in range(1, NZ):
+        go(ug.at[slot, :], ug.at[slot, :], ug_s.at[d], ug_r.at[d], at_z(d))
+    ppb[...] = (scale * dot(uslice, img[...])).astype(bf16)
+    for d in range(1, 4):
+        go(ppb, ppx.at[d], px_s.at[d], px_r.at[d], at_x(d))
+
+    def wait_lab(d, _):
+        got(labs.at[lax.rem(c + CLS - d, CLS)], lab_s.at[d], lab_r.at[d])
+        return 0
+
+    lax.fori_loop(1, CLS, wait_lab, 0)
+    lt[...] = ls_here - jnp.sum(labs[...], axis=0)
+    for d in range(1, 4):
+        go(lt, ltx.at[d], lx_s.at[d], lx_r.at[d], at_x(d))
+
 
     for h in range(2):
         ag2[h][1]()
@@ -565,9 +603,11 @@
     vm = pltpu.VMEM
     scratch = [
         vm((LEVELS, T), i32), vm((1, B), i32),
-        vm((B, E), bf16), vm((T, E), bf16), vm((N, E), bf16), vm((E, E), bf16),
+        vm((2, 4, B, E), bf16), vm((T, E), bf16), vm((N, E), bf16), vm((E, E), bf16),
         vm((16, T), i32), vm((T, E), f32), vm((T, E), bf16),
-        vm((T, B), f32), vm((T, 2 * B), bf16), vm((B, E), bf16), vm((E, 2 * B), f32), vm((T, 128), bf16),
+        vm((T, B), f32), vm((T, 2 * B), bf16), vm((E, 2 * B), f32), vm((T, 128), bf16),
+        vm((2, 4, 256, B), f32), vm((256, E), f32),
+        vm((8, 128), i32), vm((2, 4, 8, 128), i32), vm((8, 128), f32), vm((2, 4, 8, 128), f32),
         vm((8, E), bf16), vm((CLS * 8, E), bf16), vm((8, 128), i32), vm((CLS * 8, 128), i32),
         vm((8, 128), f32), vm((CLS, 8, 128), f32), vm((8, 128), f32), vm((CLS, 8, 128), f32),
         vm((8, E), bf16), vm((CLS * 8, E), bf16), vm((1, B), f32),
@@ -576,12 +616,11 @@
         vm((4, 32, E), bf16), vm((8, 128), f32), vm((4, 8, 128), f32),
         vm((8, 128), f32), vm((4, 8, 128), f32),
         vm((8, E), f32), vm((4, 8, E), f32), vm((8, E), f32), vm((4, 8, E), f32),
-        vm((T, E), bf16), vm((2, 6, 128, E), bf16), vm((2, 2, 128, E), bf16),
         vm((2, 256, E), bf16), vm((2, 6, 32, E), bf16), vm((2, 2, 32, E), bf16),
-        dma((6,)),
+        dma((7,)),
     ]
     scratch += [dma((CLS,))] * 10
-    scratch += [dma((24,))] * 2 + [dma((60,))] * 2
+    scratch += [dma((12,))] * 2 + [dma((8,))] * 4 + [dma((12,))] * 2 + [dma((60,))] * 2
     scratch += [dma((3,))] * 2 + [dma((NZ,))] * 4
     scratch += [dma((4,))] * 4 + [dma((NZ,))] * 2 + [dma((4,))] * 4
     scratch += [dma((4,))] * 4
@@ -598,7 +637,7 @@
         out_specs=[vmem] * 8,
         scratch_shapes=scratch,
         compiler_params=pltpu.CompilerParams(
-            collective_id=0, has_side_effects=True, vmem_limit_bytes=46 * 1024 * 1024
+            collective_id=0, has_side_effects=True, vmem_limit_bytes=52 * 1024 * 1024
         ),
     )(*[pltpu.with_memory_space_constraint(a, pltpu.HBM) for a in args])
     loss, gi, gt, gn, gp = pl.pallas_call(

time: 74.6 us -> 70.9 us (0.950)
  Pallas kernels: 73.8 us -> 70.1 us
    pallas_call x1, Pallas kernels: 70.4 us -> 66.7 us  [per_device(): pl.pallas_call(body, out_shape=(vm((8, 128), f32), vm((E, B), bf16), vm((...]
where the time goes in v4:
time: 70.9 us; the launch traced here: 70.8 us
  Pallas kernels  70.1 us (99%)
    pallas_call x1, Pallas kernels, per_device(): pl.pallas_call(body, out_shape=(vm((8, 128), f32), vm((E, B), bf16), vm((...  66.7 us
    pallas_call x1, Pallas kernels, per_device(): pl.pallas_call(finish, out_shape=(jax.ShapeDtypeStruct((1, 1), f32), jax....  3.48 us

profile of v4, /device:TPU:1, one launch (start us, length us, event | category | flops | bytes accessed | tf_op | source)
XLA Modules:
  0.0 70.8 jit_solution(719980786374203125)
XLA Ops:
  0.6 66.7 %shard_map.101 = (f32[8,128]{1,0:T(8,128)S(1)}, bf16[512,512]{1,0:T(8,128)(2,1)S(1)}, bf16[2048,512]{1,0:T(8,128)(2,1)S(1)}, bf16[512,2048]{1,0:T(8,128)(2,1)S(1...) custom-call(s32[7,2048]{1,0:T(8,128)} %bitcast.3, ...), custom_call_target="tpu_custom_call" | custom-call | tf_op jit(solution)/shard_map/pallas_call | solution.py:630
  67.3 3.5 %shard_map.102 = (f32[1,1]{1,0:T(1,128)}, bf16[512,512]{1,0:T(8,128)(2,1)}, bf16[2048,512]{1,0:T(8,128)(2,1)}, f32[512,512]{1,0:T(8,128)}, f32[512,512]{1,0:T(8,128)}) custom-call(f32[8,128]{1,0:T(8,128)S(1)} %get-tuple-element.18.lossb, bf16[512,512]{1,0:T(8,128)(2,1)S(1)} %get-tuple-element.19.ug, bf16[2048,512]{1,0:T(8,128)(2,1)S(1)} %get-tuple-element.20.gt, ...), custom_call_target="tpu_custom_call" | custom-call | tf_op jit(solution)/shard_map/pallas_call | solution.py:643

commit v5 on v4

--- a/solution.py
+++ b/solution.py
@@ -35,13 +35,13 @@
 
 def body(
     lin_h, lab_h, img_h, tax_h, node_h, proj_h,
-    lossb, ug, gt, cnt, pa, near_rows, sels, projo,
+    lossb, gib, gt, gnb, gpb, cnt,
     lin_ref, lab_ref, ia, tax, node, proj, lin16, base32, summed, sc32, pb, acc, remt, sall, cga, glt, gl, gst, gs,
     pub, pubs, ids, idss, stat, stats, labt, labs, far, fars, frow,
     us, ucr, uh, uzr, ppb, ppx, ppxs, ppy, lt, ltx, ltxs, lty,
     fx, fxr, fy, fyr,
-    g2, rb2, tb2,
-    in_sem,
+    g2, rb2,
+    in_sem, ug, pa, sels,
     pub_s, pub_r, ids_s, ids_r, st_s, st_r, lab_s, lab_r, far_s, far_r,
     ia_s, ia_r, gl_s, gl_r, gs_s, gs_r, rs_s, rs_r, ag_s, ag_r, uc_s, uc_r, uz_s, uz_r, ug_s, ug_r,
     px_s, px_r, py_s, py_r, pz_s, pz_r, lx_s, lx_r, ly_s, ly_r,
@@ -204,7 +204,6 @@
     remt[...] = dot_tn(rem16, jnp.where(eye, 1.0, 0.0).astype(bf16)).astype(bf16)
     for cp in loads[4:]:
         cp.wait()
-    projo[...] = proj[...]
     for q in range(4):
         glt[q : q + 1, :] = lab_ref[:, q * 128 : q * 128 + 128]
     for h in both:
@@ -267,8 +266,6 @@
     for q in range(4):
         stat[q : q + 1, :] = mtop[:, q * 128 : q * 128 + 128]
         stat[q + 4 : q + 5, :] = tot[:, q * 128 : q * 128 + 128]
-    lsum = ls8[:, 0:128] + ls8[:, 128:256] + ls8[:, 256:384] + ls8[:, 384:512]
-    labt[...] = jnp.broadcast_to(jnp.sum(lsum, keepdims=True), (8, 128))
 
     def send_stat(d):
         rc(stat, stats.at[c], st_s.at[d], st_r.at[d], at_c(d)).start()
@@ -282,6 +279,8 @@
             rc(ids, idss.at[up8(c), :], ids_s.at[d], ids_r.at[d], at_c(CLS - d)).start()
 
     peers(send_stat)
+    lsum = ls8[:, 0:128] + ls8[:, 128:256] + ls8[:, 256:384] + ls8[:, 384:512]
+    labt[...] = jnp.broadcast_to(jnp.sum(lsum, keepdims=True), (8, 128))
     stats[c] = stat[...]
     labs[c] = labt[...]
 
@@ -294,13 +293,17 @@
 
     lax.fori_loop(0, T // 512, u_block, 0)
 
-    quarter = [1024 * h + pos[h] * 256 for h in both]
-    for h in both:
+    quarter = [1024 * h + pos[h] * 64 for h in both]
+
+    def line_scores(h):
         lines[h][2]()
         lines[h][3]()
-        pr = dot(summed[rows(quarter[h], 256), :], proj[...]).astype(bf16)
+        own = jnp.concatenate([summed[rows(quarter[h] + i * 256, 64), :] for i in range(4)], axis=0)
+        pr = dot(own, proj[...]).astype(bf16)
         for j in range(4):
             sall[h, j] = scale * dot_nt(pr, ia[h, j])
+
+    line_scores(0)
 
     def wait_stat(d, _):
         got(stats.at[lax.rem(c + CLS - d, CLS)], st_s.at[d], st_r.at[d])
@@ -335,6 +338,7 @@
         go(uh.at[rows(q8(z + d) * 32, 32), :], uzr.at[z], uz_s.at[d], uz_r.at[d], at_z(d))
     uzr[z] = uh[rows(z * 32, 32), :]
 
+    line_scores(1)
     for h in both:
         for d in range(1, 4):
             got(gl.at[h, q4(pos[h] + 4 - d)], gl_s.at[h * 4 + d], gl_r.at[h * 4 + d])
@@ -346,50 +350,24 @@
     def stage(h):
         axis = 1 - h
         p = pos[axis]
-        n = 32
-        right, left = near[axis](1), near[axis](3)
-        src = g2.at[h]
-        rb = rb2.at[h]
-        tb = tb2.at[h]
-        sem = h * 6
-
-        def part(q, half):
-            return rows(q * (2 * n) + half * n, n)
-
-        def send(ref, i, dev):
-            go(ref, rb.at[i], rs_s.at[sem + i], rs_r.at[sem + i], dev)
-
-        def get(i):
-            got(rb.at[i], rs_s.at[sem + i], rs_r.at[sem + i])
-            return rb[i].astype(f32)
-
-        def own(q, half):
-            return src[part(q, half), :].astype(f32)
 
         def first():
-            send(src.at[part(q4(p + 2), 0), :], 0, right)
-            send(src.at[part(q4(p + 2), 1), :], 3, left)
-
-        def second():
-            send(src.at[part(q4(p + 1), 1), :], 1, right)
-            send(src.at[part(q4(p + 3), 0), :], 4, left)
-
-        def third():
-            tb[0] = (own(q4(p + 1), 0) + get(0)).astype(bf16)
-            send(tb.at[0], 2, right)
-            tb[1] = (own(q4(p + 3), 1) + get(3)).astype(bf16)
-            send(tb.at[1], 5, left)
+            for d in (2, 1, 3):
+                go(g2.at[h, rows(q4(p + d) * 64, 64), :], rb2.at[h, d], rs_s.at[h * 4 + d], rs_r.at[h * 4 + d], near[axis](d))
 
         def last():
-            a = own(p, 0) + get(4) + get(2)
-            b = own(p, 1) + get(1) + get(5)
-            return a.astype(bf16), b.astype(bf16)
-
-        return first, second, third, last
+            total = g2[h, rows(p * 64, 64), :].astype(f32)
+            for d in (1, 3, 2):
+                got(rb2.at[h, d], rs_s.at[h * 4 + d], rs_r.at[h * 4 + d])
+                total = total + rb2[h, d].astype(f32)
+            return total.astype(bf16)
+
+        return first, last
 
     s2 = (stage(0), stage(1))
     for h in both:
-        tid = lax.broadcasted_iota(i32, (256, 1), 0) + (tbase + quarter[h])
+        ri = lax.broadcasted_iota(i32, (256, 1), 0)
+        tid = ri + (ri >> 6) * 192 + (tbase + quarter[h])
         for j in range(4):
             t = gs[h, j]
             hit = jnp.where(tid == flat(gl[h, j], 0), 1.0, 0.0)
@@ -398,18 +376,15 @@
             cga[...] = part if j == 0 else cga[...] + part
         g2[h] = dot_nt((scale * cga[...]).astype(bf16), proj[...]).astype(bf16)
         s2[h][0]()
-        s2[h][1]()
-    for h in both:
-        s2[h][2]()
 
     def gather(h, s, blk):
         axis = (h + s) % 2
         p = pos[axis]
         right, left = near[axis](1), near[axis](3)
         if s == 0:
-            step, off, sem = 256, 1024 * h + q4(pos[1 - h] + blk) * 64, (h * 5 + blk) * 6
+            step, off, sem = 64, 1024 * h + q4(pos[1 - h] + blk) * 256, (h * 5 + blk) * 6
         else:
-            step, off, sem = 64, 1024 * h + pos[h] * 256, (h * 5 + 4) * 6
+            step, off, sem = 256, 1024 * h + pos[h] * 64, (h * 5 + 4) * 6
 
         def part(q, half):
             return gt.at[rows(off + q * step + half * 32, 32), :]
@@ -425,24 +400,11 @@
 
     ag2 = [gather(h, 1, 0) for h in range(2)]
     ag1 = [[gather(h, 0, b) for b in range(4)] for h in range(2)]
-    fsum = jnp.zeros((128, E), f32)
     for h in range(2):
-        a, b = s2[h][3]()
-        start = 1024 * h + pos[h] * 256 + pos[1 - h] * 64
-        gt[rows(start, 32), :] = a
-        gt[rows(start + 32, 32), :] = b
+        start = 1024 * h + pos[h] * 64 + pos[1 - h] * 256
+        gt[rows(start, 64), :] = s2[h][1]()
         ag2[h][0]()
         ag1[h][0][0]()
-        fsum = fsum + dot_tn(remt[rows(start, 32), :], a)
-        fsum = fsum + dot_tn(remt[rows(start + 32, 32), :], b)
-    far[...] = fsum[0:8].astype(bf16)
-
-    def send_far(d):
-        @pl.when(c >= d)
-        def _():
-            rc(far, fars.at[up8(c), :], far_s.at[d], far_r.at[d], at_c(CLS - d)).start()
-
-    peers(send_far)
     for d in range(1, NZ):
         got(uzr.at[q8(z + NZ - d)], uz_s.at[d], uz_r.at[d])
     uslice = uzr[0].astype(f32)
@@ -457,6 +419,19 @@
     for d in range(1, 4):
         go(ppb, ppx.at[d], px_s.at[d], px_r.at[d], at_x(d))
 
+    fsum = jnp.zeros((128, E), f32)
+    for h in both:
+        r = rows(quarter[h] + pos[1 - h] * 256, 64)
+        fsum = fsum + dot_tn(remt[r, :], gt[r, :])
+    far[...] = fsum[0:8].astype(bf16)
+
+    def send_far(d):
+        @pl.when(c >= d)
+        def _():
+            rc(far, fars.at[up8(c), :], far_s.at[d], far_r.at[d], at_c(CLS - d)).start()
+
+    peers(send_far)
+
     def wait_lab(d, _):
         got(labs.at[lax.rem(c + CLS - d, CLS)], lab_s.at[d], lab_r.at[d])
         return 0
@@ -490,26 +465,6 @@
     for h in range(2):
         ag2[h][3]()
         ag1[h][2][0]()
-
-    def wait_far(d, _):
-        @pl.when(c + d < CLS)
-        def _():
-            got(idss.at[up8(c + d), :], ids_s.at[d], ids_r.at[d])
-            got(fars.at[up8(c + d), :], far_s.at[d], far_r.at[d])
-        return 0
-
-    lax.fori_loop(1, CLS, wait_far, 0)
-    ri = lax.broadcasted_iota(i32, (128, 128), 0)
-    ci = lax.broadcasted_iota(i32, (128, 128), 1)
-    idrow = jnp.max(jnp.where(ri == ci, idss[...], -1), axis=0, keepdims=True)
-    match = (last == idrow) & (last >= 0)
-    fx[...] = dot(jnp.where(match, 1.0, 0.0).astype(bf16), fars[...])[0:8]
-    for d in range(1, 4):
-        go(fx, fxr.at[d], fx_s.at[d], fx_r.at[d], at_x(d))
-
-    for d in range(1, NZ):
-        got(ug.at[rows((k * 8 + q8(z + NZ - d)) * 32, 32), :], ug_s.at[d], ug_r.at[d])
-    go(ug.at[mine, :], ug.at[mine, :], uc_s.at[1], uc_r.at[1], mate)
 
     for d in range(1, 4):
         got(ppy.at[d], py_s.at[d], py_r.at[d])
@@ -525,28 +480,59 @@
     for b in (3, 1):
         for h in range(2):
             ag1[h][b][1]()
+    def wait_far(d, _):
+        @pl.when(c + d < CLS)
+        def _():
+            got(idss.at[up8(c + d), :], ids_s.at[d], ids_r.at[d])
+            got(fars.at[up8(c + d), :], far_s.at[d], far_r.at[d])
+        return 0
+
+    lax.fori_loop(1, CLS, wait_far, 0)
+    ri = lax.broadcasted_iota(i32, (128, 128), 0)
+    ci = lax.broadcasted_iota(i32, (128, 128), 1)
+    idrow = jnp.max(jnp.where(ri == ci, idss[...], -1), axis=0, keepdims=True)
+    match = (last == idrow) & (last >= 0)
+    fx[...] = dot(jnp.where(match, 1.0, 0.0).astype(bf16), fars[...])[0:8]
+    for d in range(1, 4):
+        go(fx, fxr.at[d], fx_s.at[d], fx_r.at[d], at_x(d))
+
+    for h in range(2):
+        ag1[h][2][1]()
+
+    for d in range(1, NZ):
+        got(ug.at[rows((k * 8 + q8(z + NZ - d)) * 32, 32), :], ug_s.at[d], ug_r.at[d])
+    go(ug.at[mine, :], ug.at[mine, :], uc_s.at[1], uc_r.at[1], mate)
+
     for d in range(1, 4):
         got(fxr.at[d], fx_s.at[d], fx_r.at[d])
     fy[...] = fx[...] + fxr[1] + fxr[2] + fxr[3]
     for d in range(1, 4):
         go(fy, fyr.at[d], fy_s.at[d], fy_r.at[d], at_y(d))
-    for h in range(2):
-        ag1[h][2][1]()
-
+    def add_rows(b):
+        for h in both:
+            ag1[h][b][2]()
+            ag1[h][b][3]()
+
+    add_rows(0)
     got(ug.at[other, :], uc_s.at[1], uc_r.at[1])
+    gib[...] = (scale * dot_tn(ug[...], proj[...])).astype(bf16)
 
     for d in range(1, NZ):
         got(pa.at[rows((k * 8 + q8(z + NZ - d)) * 32, 32), :], pz_s.at[d], pz_r.at[d])
     go(pa.at[mine, :], pa.at[mine, :], uc_s.at[2], uc_r.at[2], mate)
 
+    add_rows(3)
+    add_rows(1)
     for d in range(1, 4):
         got(fyr.at[d], fy_s.at[d], fy_r.at[d])
-    near_rows[...] = fy[...] + fyr[1] + fyr[2] + fyr[3]
-    for b in (0, 3, 1, 2):
-        for h in range(2):
-            ag1[h][b][2]()
-            ag1[h][b][3]()
+    own = fy[...] + fyr[1] + fyr[2] + fyr[3]
+    own = jnp.concatenate([own, jnp.zeros_like(own)], axis=0)
+    hi = own.astype(bf16)
+    lo = (own - hi.astype(f32)).astype(bf16)
+    gnb[...] = dot_tn(sels[...], hi) + dot_tn(sels[...], lo)
+    add_rows(2)
     got(pa.at[other, :], uc_s.at[2], uc_r.at[2])
+    gpb[...] = pa[...].astype(f32)
 
     for cp in started:
         cp.wait_send()
@@ -569,27 +555,19 @@
     lax.fori_loop(1, CLS, drain, 0)
 
 
-def finish(lossb, ug, gt, cnt, pa, near_rows, sels, proj, loss_o, gi_o, gt_o, gn_o, gp_o, gib, gnb, gpb, sem):
-    outs = [pltpu.make_async_copy(gt, gt_o, sem.at[0])]
-    outs[-1].start()
-    gpb[...] = pa[...].astype(f32)
-    outs.append(pltpu.make_async_copy(gpb, gp_o, sem.at[1]))
-    outs[-1].start()
-    own = near_rows[...]
-    own = jnp.concatenate([own, jnp.zeros_like(own)], axis=0)
-    hi = own.astype(bf16)
-    lo = (own - hi.astype(f32)).astype(bf16)
-    sel = sels[...]
+def finish(lossb, gi, gt, gn, gp, cnt, loss_o, gi_o, gt_o, gn_o, gp_o, gnb, sem):
+    outs = [
+        pltpu.make_async_copy(a, b, sem.at[i])
+        for i, (a, b) in enumerate(((gt, gt_o), (gp, gp_o), (gi, gi_o)))
+    ]
+    for cp in outs:
+        cp.start()
+    loss_o[...] = lossb[0:1, 0:1]
     for i in range(2):
         r = slice(i * 256, i * 256 + 256)
-        at = sel[:, r]
-        gnb[r, :] = dot(cnt[r, :], gt[...]) + dot_tn(at, hi) + dot_tn(at, lo)
-        outs.append(pltpu.make_async_copy(gnb.at[r, :], gn_o.at[r, :], sem.at[2 + i]))
+        gnb[r, :] = gn[r, :] + dot(cnt[r, :], gt[...])
+        outs.append(pltpu.make_async_copy(gnb.at[r, :], gn_o.at[r, :], sem.at[3 + i]))
         outs[-1].start()
-    gib[...] = (scale * dot_tn(ug[...], proj[...])).astype(bf16)
-    outs.append(pltpu.make_async_copy(gib, gi_o, sem.at[4]))
-    outs[-1].start()
-    loss_o[...] = lossb[0:1, 0:1]
     for cp in outs:
         cp.wait()
 
@@ -616,8 +594,8 @@
         vm((4, 32, E), bf16), vm((8, 128), f32), vm((4, 8, 128), f32),
         vm((8, 128), f32), vm((4, 8, 128), f32),
         vm((8, E), f32), vm((4, 8, E), f32), vm((8, E), f32), vm((4, 8, E), f32),
-        vm((2, 256, E), bf16), vm((2, 6, 32, E), bf16), vm((2, 2, 32, E), bf16),
-        dma((7,)),
+        vm((2, 256, E), bf16), vm((2, 4, 64, E), bf16),
+        dma((7,)), vm((E, B), bf16), vm((E, E), bf16), vm((16, N), bf16),
     ]
     scratch += [dma((CLS,))] * 10
     scratch += [dma((12,))] * 2 + [dma((8,))] * 4 + [dma((12,))] * 2 + [dma((60,))] * 2
@@ -630,11 +608,11 @@
     held = pl.pallas_call(
         body,
         out_shape=(
-            vm((8, 128), f32), vm((E, B), bf16), vm((T, E), bf16), vm((N, T), bf16),
-            vm((E, E), bf16), vm((8, E), f32), vm((16, N), bf16), vm((E, E), bf16),
+            vm((8, 128), f32), vm((B, E), bf16), vm((T, E), bf16), vm((N, E), f32), vm((E, E), f32),
+            vm((N, T), bf16),
         ),
         in_specs=[hbm] * 6,
-        out_specs=[vmem] * 8,
+        out_specs=[vmem] * 6,
         scratch_shapes=scratch,
         compiler_params=pltpu.CompilerParams(
             collective_id=0, has_side_effects=True, vmem_limit_bytes=52 * 1024 * 1024
@@ -649,10 +627,10 @@
             jax.ShapeDtypeStruct((N, E), f32),
             jax.ShapeDtypeStruct((E, E), f32),
         ),
-        in_specs=[vmem] * 8,
+        in_specs=[vmem] * 6,
         out_specs=[vmem] + [hbm] * 4,
-        scratch_shapes=[vm((B, E), bf16), vm((N, E), f32), vm((E, E), f32), dma((5,))],
-        compiler_params=pltpu.CompilerParams(vmem_limit_bytes=12 * 1024 * 1024),
+        scratch_shapes=[vm((N, E), f32), dma((5,))],
+        compiler_params=pltpu.CompilerParams(vmem_limit_bytes=8 * 1024 * 1024),
     )(*held)
     return (loss.reshape(()), gi, gt, gn, gp)
 

time: 70.9 us -> 69.1 us (0.975)
  Pallas kernels: 70.1 us -> 67.7 us
    pallas_call x1, Pallas kernels: 66.7 us -> 64.7 us  [per_device(): pl.pallas_call(body, out_shape=(vm((8, 128), f32), vm((B, E), bf16), vm((...]
where the time goes in v5:
time: 69.1 us; the launch traced here: 68.4 us
  Pallas kernels  67.7 us (98%)
    pallas_call x1, Pallas kernels, per_device(): pl.pallas_call(body, out_shape=(vm((8, 128), f32), vm((B, E), bf16), vm((...  64.7 us
    pallas_call x1, Pallas kernels, per_device(): pl.pallas_call(finish, out_shape=(jax.ShapeDtypeStruct((1, 1), f32), jax....  3.02 us

profile of v5, /device:TPU:1, one launch (start us, length us, event | category | flops | bytes accessed | tf_op | source)
XLA Modules:
  0.0 68.4 jit_solution(10721436428299415352)
XLA Ops:
  0.6 64.7 %shard_map.101 = (f32[8,128]{1,0:T(8,128)S(1)}, bf16[512,512]{1,0:T(8,128)(2,1)S(1)}, bf16[2048,512]{1,0:T(8,128)(2,1)S(1)}, f32[512,512]{1,0:T(8,128)S(1)}, f32...) custom-call(s32[7,2048]{1,0:T(8,128)} %bitcast.3, s32[1,512]{1,0:T(1,128)} %bitcast.4, bf16[512,512]{1,0:T(8,128)(2,1)} %img_h.1, ...), custom_call_target="tpu_custom_call" | custom-call | tf_op jit(solution)/shard_map/pallas_call | solution.py:608
  65.4 3.0 %shard_map.102 = (f32[1,1]{1,0:T(1,128)}, bf16[512,512]{1,0:T(8,128)(2,1)}, bf16[2048,512]{1,0:T(8,128)(2,1)}, f32[512,512]{1,0:T(8,128)}, f32[512,512]{1,0:T(8,128)}) custom-call(f32[8,128]{1,0:T(8,128)S(1)} %get-tuple-element.16.lossb, bf16[512,512]{1,0:T(8,128)(2,1)S(1)} %get-tuple-element.17.gi, bf16[2048,512]{1,0:T(8,128)(2,1)S(1)} %get-tuple-element.18.gt, ...), custom_call_target="tpu_custom_call" | custom-call | tf_op jit(solution)/shard_map/pallas_call | solution.py:621

commit v6 on v5

--- a/solution.py
+++ b/solution.py
@@ -376,6 +376,18 @@
             cga[...] = part if j == 0 else cga[...] + part
         g2[h] = dot_nt((scale * cga[...]).astype(bf16), proj[...]).astype(bf16)
         s2[h][0]()
+    fsum = jnp.zeros((128, E), f32)
+    for h in both:
+        for i in range(4):
+            fsum = fsum + dot_tn(remt[rows(quarter[h] + i * 256, 64), :], g2[h, i * 64 : i * 64 + 64, :])
+    far[...] = fsum[0:8].astype(bf16)
+
+    def send_far(d):
+        @pl.when(c >= d)
+        def _():
+            rc(far, fars.at[up8(c), :], far_s.at[d], far_r.at[d], at_c(CLS - d)).start()
+
+    peers(send_far)
 
     def gather(h, s, blk):
         axis = (h + s) % 2
@@ -419,19 +431,6 @@
     for d in range(1, 4):
         go(ppb, ppx.at[d], px_s.at[d], px_r.at[d], at_x(d))
 
-    fsum = jnp.zeros((128, E), f32)
-    for h in both:
-        r = rows(quarter[h] + pos[1 - h] * 256, 64)
-        fsum = fsum + dot_tn(remt[r, :], gt[r, :])
-    far[...] = fsum[0:8].astype(bf16)
-
-    def send_far(d):
-        @pl.when(c >= d)
-        def _():
-            rc(far, fars.at[up8(c), :], far_s.at[d], far_r.at[d], at_c(CLS - d)).start()
-
-    peers(send_far)
-
     def wait_lab(d, _):
         got(labs.at[lax.rem(c + CLS - d, CLS)], lab_s.at[d], lab_r.at[d])
         return 0
@@ -441,6 +440,22 @@
     for d in range(1, 4):
         go(lt, ltx.at[d], lx_s.at[d], lx_r.at[d], at_x(d))
 
+
+    def wait_far(d, _):
+        @pl.when(c + d < CLS)
+        def _():
+            got(idss.at[up8(c + d), :], ids_s.at[d], ids_r.at[d])
+            got(fars.at[up8(c + d), :], far_s.at[d], far_r.at[d])
+        return 0
+
+    lax.fori_loop(1, CLS, wait_far, 0)
+    ri = lax.broadcasted_iota(i32, (128, 128), 0)
+    ci = lax.broadcasted_iota(i32, (128, 128), 1)
+    idrow = jnp.max(jnp.where(ri == ci, idss[...], -1), axis=0, keepdims=True)
+    match = (last == idrow) & (last >= 0)
+    fx[...] = dot(jnp.where(match, 1.0, 0.0).astype(bf16), fars[...])[0:8]
+    for d in range(1, 4):
+        go(fx, fxr.at[d], fx_s.at[d], fx_r.at[d], at_x(d))
 
     for h in range(2):
         ag2[h][1]()
@@ -457,6 +472,11 @@
     for d in range(1, 4):
         go(ppxs, ppy.at[d], py_s.at[d], py_r.at[d], at_y(d))
         go(ltxs, lty.at[d], ly_s.at[d], ly_r.at[d], at_y(d))
+    for d in range(1, 4):
+        got(fxr.at[d], fx_s.at[d], fx_r.at[d])
+    fy[...] = fx[...] + fxr[1] + fxr[2] + fxr[3]
+    for d in range(1, 4):
+        go(fy, fyr.at[d], fy_s.at[d], fy_r.at[d], at_y(d))
 
     for h in range(2):
         ag2[h][2]()
@@ -480,22 +500,6 @@
     for b in (3, 1):
         for h in range(2):
             ag1[h][b][1]()
-    def wait_far(d, _):
-        @pl.when(c + d < CLS)
-        def _():
-            got(idss.at[up8(c + d), :], ids_s.at[d], ids_r.at[d])
-            got(fars.at[up8(c + d), :], far_s.at[d], far_r.at[d])
-        return 0
-
-    lax.fori_loop(1, CLS, wait_far, 0)
-    ri = lax.broadcasted_iota(i32, (128, 128), 0)
-    ci = lax.broadcasted_iota(i32, (128, 128), 1)
-    idrow = jnp.max(jnp.where(ri == ci, idss[...], -1), axis=0, keepdims=True)
-    match = (last == idrow) & (last >= 0)
-    fx[...] = dot(jnp.where(match, 1.0, 0.0).astype(bf16), fars[...])[0:8]
-    for d in range(1, 4):
-        go(fx, fxr.at[d], fx_s.at[d], fx_r.at[d], at_x(d))
-
     for h in range(2):
         ag1[h][2][1]()
 
@@ -503,11 +507,6 @@
         got(ug.at[rows((k * 8 + q8(z + NZ - d)) * 32, 32), :], ug_s.at[d], ug_r.at[d])
     go(ug.at[mine, :], ug.at[mine, :], uc_s.at[1], uc_r.at[1], mate)
 
-    for d in range(1, 4):
-        got(fxr.at[d], fx_s.at[d], fx_r.at[d])
-    fy[...] = fx[...] + fxr[1] + fxr[2] + fxr[3]
-    for d in range(1, 4):
-        go(fy, fyr.at[d], fy_s.at[d], fy_r.at[d], at_y(d))
     def add_rows(b):
         for h in both:
             ag1[h][b][2]()

time: 69.1 us -> 68.9 us (level)
  no operation moved by 1% of the time
where the time goes in v6:
time: 68.9 us; the launch traced here: 68.8 us
  Pallas kernels  68.2 us (99%)
    pallas_call x1, Pallas kernels, per_device(): pl.pallas_call(body, out_shape=(vm((8, 128), f32), vm((B, E), bf16), vm((...  65.2 us
    pallas_call x1, Pallas kernels, per_device(): pl.pallas_call(finish, out_shape=(jax.ShapeDtypeStruct((1, 1), f32), jax....  3.02 us

profile of v6, /device:TPU:1, one launch (start us, length us, event | category | flops | bytes accessed | tf_op | source)
XLA Modules:
  0.0 68.8 jit_solution(2254215960444688968)
XLA Ops:
  0.6 65.2 %shard_map.101 = (f32[8,128]{1,0:T(8,128)S(1)}, bf16[512,512]{1,0:T(8,128)(2,1)S(1)}, bf16[2048,512]{1,0:T(8,128)(2,1)S(1)}, f32[512,512]{1,0:T(8,128)S(1)}, f32...) custom-call(s32[7,2048]{1,0:T(8,128)} %bitcast.3, s32[1,512]{1,0:T(1,128)} %bitcast.4, bf16[512,512]{1,0:T(8,128)(2,1)} %img_h.1, ...), custom_call_target="tpu_custom_call" | custom-call | tf_op jit(solution)/shard_map/pallas_call | solution.py:607
  65.8 3.0 %shard_map.102 = (f32[1,1]{1,0:T(1,128)}, bf16[512,512]{1,0:T(8,128)(2,1)}, bf16[2048,512]{1,0:T(8,128)(2,1)}, f32[512,512]{1,0:T(8,128)}, f32[512,512]{1,0:T(8,128)}) custom-call(f32[8,128]{1,0:T(8,128)S(1)} %get-tuple-element.16.lossb, bf16[512,512]{1,0:T(8,128)(2,1)S(1)} %get-tuple-element.17.gi, bf16[2048,512]{1,0:T(8,128)(2,1)S(1)} %get-tuple-element.18.gt, ...), custom_call_target="tpu_custom_call" | custom-call | tf_op jit(solution)/shard_map/pallas_call | solution.py:620

commit v7 on v6

--- a/solution.py
+++ b/solution.py
@@ -221,6 +221,13 @@
     for h in both:
         lines[h][1]()
 
+    def send_ids(d):
+        @pl.when(c >= d)
+        def _():
+            rc(ids, idss.at[up8(c), :], ids_s.at[d], ids_r.at[d], at_c(CLS - d)).start()
+
+    peers(send_ids)
+
     def wait_pub(d, _):
         @pl.when(c >= d)
         def _():
@@ -273,11 +280,6 @@
     def send_lab(d):
         rc(labt, labs.at[c], lab_s.at[d], lab_r.at[d], at_c(d)).start()
 
-    def send_ids(d):
-        @pl.when(c >= d)
-        def _():
-            rc(ids, idss.at[up8(c), :], ids_s.at[d], ids_r.at[d], at_c(CLS - d)).start()
-
     peers(send_stat)
     lsum = ls8[:, 0:128] + ls8[:, 128:256] + ls8[:, 256:384] + ls8[:, 384:512]
     labt[...] = jnp.broadcast_to(jnp.sum(lsum, keepdims=True), (8, 128))
@@ -292,6 +294,7 @@
         return 0
 
     lax.fori_loop(0, T // 512, u_block, 0)
+    peers(send_lab)
 
     quarter = [1024 * h + pos[h] * 64 for h in both]
 
@@ -329,8 +332,6 @@
     mine = rows(k * 256, 256)
     uc = go(us.at[other, :], ucr, uc_s.at[0], uc_r.at[0], mate)
 
-    peers(send_ids)
-    peers(send_lab)
 
     got(ucr, uc_s.at[0], uc_r.at[0])
     uh[...] = (us[mine, :].astype(f32) + ucr[...].astype(f32)).astype(bf16)

time: 68.9 us -> 68.7 us (level)
  no operation moved by 1% of the time
where the time goes in v7:
time: 68.7 us; the launch traced here: 68.6 us
  Pallas kernels  68 us (99%)
    pallas_call x1, Pallas kernels, per_device(): pl.pallas_call(body, out_shape=(vm((8, 128), f32), vm((B, E), bf16), vm((...  65 us
    pallas_call x1, Pallas kernels, per_device(): pl.pallas_call(finish, out_shape=(jax.ShapeDtypeStruct((1, 1), f32), jax....  3.02 us

profile of v7, /device:TPU:1, one launch (start us, length us, event | category | flops | bytes accessed | tf_op | source)
XLA Modules:
  0.0 68.6 jit_solution(979775380413992035)
XLA Ops:
  0.6 65.0 %shard_map.101 = (f32[8,128]{1,0:T(8,128)S(1)}, bf16[512,512]{1,0:T(8,128)(2,1)S(1)}, bf16[2048,512]{1,0:T(8,128)(2,1)S(1)}, f32[512,512]{1,0:T(8,128)S(1)}, f32...) custom-call(s32[7,2048]{1,0:T(8,128)} %bitcast.3, s32[1,512]{1,0:T(1,128)} %bitcast.4, bf16[512,512]{1,0:T(8,128)(2,1)} %img_h.1, ...), custom_call_target="tpu_custom_call" | custom-call | tf_op jit(solution)/shard_map/pallas_call | solution.py:608
  65.6 3.0 %shard_map.102 = (f32[1,1]{1,0:T(1,128)}, bf16[512,512]{1,0:T(8,128)(2,1)}, bf16[2048,512]{1,0:T(8,128)(2,1)}, f32[512,512]{1,0:T(8,128)}, f32[512,512]{1,0:T(8,128)}) custom-call(f32[8,128]{1,0:T(8,128)S(1)} %get-tuple-element.16.lossb, bf16[512,512]{1,0:T(8,128)(2,1)S(1)} %get-tuple-element.17.gi, bf16[2048,512]{1,0:T(8,128)(2,1)S(1)} %get-tuple-element.18.gt, ...), custom_call_target="tpu_custom_call" | custom-call | tf_op jit(solution)/shard_map/pallas_call | solution.py:621
